TPU v7x, 256 devices: a whole 4x4x8 slice. The times are simulated.
256 devices in a mesh: section: 2 (over core), req: 16 (over x, y), head: 8 (over z).
Axes of the slice: x: 4, y: 4, z: 8, core: 2. Of those that a mesh axis runs over, the one named last changes fastest.
Arguments:
- tokens: bfloat16 [256, 8192], P(None, 'req'), may hold values from -14 to 14
- attention_gain: bfloat16 [2, 8192], P('section', 'req'), may hold values from 0.099609375 to 1.8984375
- query_key_value_weight: bfloat16 [2, 8192, 8, 1280], P('section', 'req', 'head'), may hold values from -0.0625 to 0.0625
- head_output_weight: bfloat16 [2, 8, 1024, 8192], P('section', 'head', None, 'req'), may hold values from -0.0625 to 0.0625
- feedforward_gain: bfloat16 [2, 8192], P('section', 'req'), may hold values from 0.099609375 to 1.8984375
- gate_up: bfloat16 [2, 8192, 2, 14336], P('section', 'req', None, 'head'), may hold values from -0.0625 to 0.0625
- down_weight: bfloat16 [2, 14336, 8192], P('section', 'head', 'req'), may hold values from -0.046875 to 0.046875
- packed_cache: bfloat16 [2, 32768, 8, 256], P('section', 'req', 'head'), may hold values from -70 to 70
- long_cache: bfloat16 [2, 2, 32768, 8, 256], P('section', None, 'req', 'head'), may hold values from -70 to 70
- lengths: int32 [16, 16], P('req'), may hold values from 1 to 256, 2048 in all within a row
- long_split: int32 [2, 16], P(None, 'req'), may hold values from 1 to 2048, 16384 in all within a row
Outputs:
- layer_outputs: bfloat16 [2, 256, 8192], P('section', None, 'req')
Inputs may be any that keep to these rules, and one draw needn't show every extreme that they name: Row g holds the lengths of the 16 requests of request group g in order; they sum to 2048, and the requests' keys fill that group's 2048 slots of packed_cache one request after another. `long_split`: entry (j, g) counts the live slots, the first ones, of group g's 2048 slots of long request j; each row sums to 16384.
All inputs are finite; a program needn't handle non-finite values.
Results may differ from a plain program's by a relative error of at most 0.04.
Values may be sent and summed in bfloat16 or wider, within the bound.
A program may use at most 64 MiB of HBM per device.

v0:
```python
import math

import jax
import jax.numpy as jnp
from jax import lax
from jax.sharding import PartitionSpec as P

MODEL_WIDTH = 8192
QUERY_HEADS = 64
KEY_VALUE_HEADS = 8
HEAD_SIZE = 128
LONG = 16384


EPSILON = 1e-05


def merged(part, axis, combine):
    gathered = jax.tree.map(lambda a: lax.all_gather(a, axis), part)

    def take(source):
        return jax.tree.map(lambda a: lax.dynamic_index_in_dim(a, source, 0, False), gathered)

    return lax.fori_loop(
        1, lax.axis_size(axis), lambda source, state: combine(state, take(source)), take(0)
    )


def shifted(value, axis, by):
    peers = lax.axis_size(axis)
    pairs = [(i, i + by) for i in range(peers) if 0 <= i + by < peers]
    return lax.ppermute(value, axis, pairs)


def rotate(values, position):
    half_dim = values.shape[-1] // 2
    freq_ids = jnp.arange(half_dim).astype(jnp.float32)
    inverse = 1.0 / 10000.0 ** (freq_ids * 2.0 / values.shape[-1])
    angles = position.astype(jnp.float32)[:, None] * inverse[None, :]
    cosine = jnp.cos(angles)[:, None, None, :]
    sine_part = jnp.sin(angles)[:, None, None, :]
    lower_half = values[..., :half_dim]
    upper_half = values[..., half_dim:]
    return jnp.concatenate(
        [
            lower_half * cosine - upper_half * sine_part,
            upper_half * cosine + lower_half * sine_part,
        ],
        -1,
    )


def add_pair(earlier, second_part):
    return earlier + second_part


def combine_partial(earlier, second_part):
    peak = jnp.maximum(earlier[0], second_part[0])
    left_factor = jnp.exp(earlier[0] - peak)
    right_factor = jnp.exp(second_part[0] - peak)
    softmax_total = earlier[1] * left_factor + second_part[1] * right_factor
    weighted_sum = earlier[2] * left_factor[..., None] + second_part[2] * right_factor[..., None]
    return (peak, softmax_total, weighted_sum)


def over_requests(values, combiner):
    return merged(values, "req", combiner)


def rows_apply(values, row_fn):
    return row_fn(lax.all_gather(values, "req", axis=0, tiled=True), jnp.int32(0))


def rows_project(term_fn, row_count):
    return lax.psum_scatter(
        term_fn(jnp.int32(0), row_count * lax.axis_size("req")),
        "req",
        scatter_dimension=0,
        tiled=True,
    )


def head_total(values):
    return lax.psum(values, "head")


def keep_rows(piece_rows, start_row):
    return piece_rows


def norm_rows(values, gain_row):
    floats = values.astype(jnp.float32)
    squares = over_requests(jnp.sum(floats * floats, axis=-1), add_pair)
    return (
        floats * lax.rsqrt(squares / MODEL_WIDTH + EPSILON)[:, None] * gain_row.astype(jnp.float32)
    ).astype(jnp.bfloat16)


def decoder_layer(
    inputs,
    micro_batch,
    attention_gain,
    query_key_value_weight,
    head_output_weight,
    feedforward_gain,
    gate_up,
    down_weight,
    packed_cache,
    long_cache,
    lengths,
    long_split,
):
    req_count = lax.axis_size("req")
    group_index = lax.axis_index("req")
    blocks = inputs.shape[0] // req_count
    columns = query_key_value_weight.shape[1]
    kv_local = query_key_value_weight.shape[2]
    requests_per_group = QUERY_HEADS // KEY_VALUE_HEADS
    score_scale = 1.0 / math.sqrt(HEAD_SIZE)
    normalized_input = norm_rows(inputs, attention_gain[0])
    in_weights = query_key_value_weight[0].reshape(
        columns, kv_local * (requests_per_group + 2) * HEAD_SIZE
    )

    def qkv_term(start_row, row_count):
        return jnp.dot(normalized_input, in_weights, preferred_element_type=jnp.float32)

    projected_rows = rows_project(qkv_term, blocks).reshape(
        blocks, kv_local, requests_per_group + 2, HEAD_SIZE
    )
    local_rows = jnp.arange(blocks)
    row_lengths = lengths[0]
    owner_long = (group_index == 0) | (group_index == req_count // 2)
    long_row = (local_rows == 0) & (micro_batch == 0) & owner_long
    position = row_lengths + jnp.where(long_row, LONG, 0).astype(jnp.int32)
    queries = rotate(projected_rows[:, :, :requests_per_group], position).astype(jnp.bfloat16)
    new_key = rotate(projected_rows[:, :, requests_per_group : requests_per_group + 1], position)[
        :, :, 0
    ].astype(jnp.bfloat16)
    new_value = projected_rows[:, :, requests_per_group + 1].astype(jnp.bfloat16)
    gathered = rows_apply(
        queries[0:1].reshape(1, kv_local * requests_per_group * HEAD_SIZE), keep_rows
    )
    long_queries = jnp.stack([gathered[0], gathered[req_count // 2]]).reshape(
        2, kv_local, requests_per_group, HEAD_SIZE
    )
    far_cache = long_cache[0]
    far_live = (jnp.arange(far_cache.shape[1])[None, :] < long_split[:, 0][:, None])[
        :, None, None, :
    ]
    far_scores = (
        jnp.einsum(
            "jkhd,jpkd->jkhp",
            long_queries,
            far_cache[..., :HEAD_SIZE],
            preferred_element_type=jnp.float32,
        )
        * score_scale
    )
    far_max = jnp.max(jnp.where(far_live, far_scores, -jnp.inf), axis=-1)
    far_weights = jnp.where(
        far_live, jnp.exp(jnp.where(far_live, far_scores - far_max[..., None], 0.0)), 0.0
    ).astype(jnp.bfloat16)
    far_totals = jnp.sum(far_weights.astype(jnp.float32), axis=-1)
    far_summed = jnp.einsum(
        "jkhp,jpkd->jkhd",
        far_weights,
        far_cache[..., HEAD_SIZE:],
        preferred_element_type=jnp.float32,
    )
    far_max, far_totals, far_summed = over_requests(
        (far_max, far_totals, far_summed), combine_partial
    )
    far_index = jnp.where(group_index == 0, 0, 1)
    chosen_max = lax.dynamic_index_in_dim(far_max, far_index, 0, keepdims=False)
    chosen_totals = lax.dynamic_index_in_dim(far_totals, far_index, 0, keepdims=False)
    chosen_summed = lax.dynamic_index_in_dim(far_summed, far_index, 0, keepdims=False)
    pack_part = packed_cache[0]
    seg_ends = jnp.cumsum(lengths[0])
    slot_ids = jnp.arange(pack_part.shape[0])
    slot_owner = jnp.sum((slot_ids[:, None] >= seg_ends[None, :]).astype(jnp.int32), axis=1)
    request_ids = micro_batch * blocks + local_rows
    in_segment = (slot_owner[None, :] == request_ids[:, None])[:, None, None, :]
    scores = (
        jnp.einsum(
            "rkhd,pkd->rkhp",
            queries,
            pack_part[..., :HEAD_SIZE],
            preferred_element_type=jnp.float32,
        )
        * score_scale
    )
    own_score = (
        jnp.einsum("rkhd,rkd->rkh", queries, new_key, preferred_element_type=jnp.float32)
        * score_scale
    )
    row_max = jnp.maximum(jnp.max(jnp.where(in_segment, scores, -jnp.inf), axis=-1), own_score)
    long_mask = long_row[:, None, None]
    row_max = jnp.where(long_mask, jnp.maximum(row_max, chosen_max[None]), row_max)
    weights = jnp.where(
        in_segment, jnp.exp(jnp.where(in_segment, scores - row_max[..., None], 0.0)), 0.0
    ).astype(jnp.bfloat16)
    own_weights = jnp.exp(own_score - row_max).astype(jnp.bfloat16)
    far_factor = jnp.where(
        long_mask, jnp.exp(jnp.where(long_mask, chosen_max[None] - row_max, 0.0)), 0.0
    )
    softmax_total = (
        jnp.sum(weights.astype(jnp.float32), axis=-1)
        + own_weights.astype(jnp.float32)
        + far_factor * chosen_totals[None]
    )
    weighted_sum = jnp.einsum(
        "rkhp,pkd->rkhd", weights, pack_part[..., HEAD_SIZE:], preferred_element_type=jnp.float32
    )
    weighted_sum = (
        weighted_sum
        + own_weights.astype(jnp.float32)[..., None] * new_value.astype(jnp.float32)[:, :, None, :]
    )
    weighted_sum = weighted_sum + far_factor[..., None] * chosen_summed[None]
    attended_heads = (
        (weighted_sum / softmax_total[..., None])
        .astype(jnp.bfloat16)
        .reshape(blocks, kv_local * requests_per_group * HEAD_SIZE)
    )
    out_weights = head_output_weight[0].reshape(kv_local * requests_per_group * HEAD_SIZE, columns)

    def project_heads(piece_rows, start_row):
        return jnp.dot(piece_rows, out_weights, preferred_element_type=jnp.float32)

    attended = head_total(rows_apply(attended_heads, project_heads))
    residual = (inputs.astype(jnp.float32) + attended).astype(jnp.bfloat16)
    normed_two = norm_rows(residual, feedforward_gain[0])
    ff_weights = gate_up[0].reshape(columns, -1)

    def ff_term(start_row, row_count):
        return jnp.dot(normed_two, ff_weights, preferred_element_type=jnp.float32)

    gate_and_up = rows_project(ff_term, blocks)
    hidden_width = gate_and_up.shape[1] // 2
    hidden = (jax.nn.silu(gate_and_up[:, :hidden_width]) * gate_and_up[:, hidden_width:]).astype(
        jnp.bfloat16
    )
    lower_weights = down_weight[0]

    def project_hidden(piece_rows, start_row):
        return jnp.dot(piece_rows, lower_weights, preferred_element_type=jnp.float32)

    lowered = head_total(rows_apply(hidden, project_hidden))
    return (residual.astype(jnp.float32) + lowered).astype(jnp.bfloat16)


def local(
    tokens,
    attention_gain,
    query_key_value_weight,
    head_output_weight,
    feedforward_gain,
    gate_up,
    down_weight,
    packed_cache,
    long_cache,
    lengths,
    long_split,
):
    req_count = lax.axis_size("req")
    section_index = lax.axis_index("section")
    batch_count = 1
    per_group = tokens.shape[0] // req_count
    blocks = per_group // batch_count
    columns = tokens.shape[1]
    token_grid = tokens.reshape(req_count, per_group, columns)
    result = jnp.zeros_like(token_grid)
    incoming = jnp.zeros((req_count * blocks, columns), jnp.bfloat16)
    for phase_step in range(batch_count + 1):
        micro_batch = phase_step - section_index
        is_active = (micro_batch >= 0) & (micro_batch < batch_count)
        micro_batch = jnp.clip(micro_batch, 0, batch_count - 1)
        new_batch = token_grid.reshape(req_count * blocks, columns)
        inputs = jnp.where(section_index == 0, new_batch, incoming)
        output = decoder_layer(
            inputs,
            micro_batch,
            attention_gain,
            query_key_value_weight,
            head_output_weight,
            feedforward_gain,
            gate_up,
            down_weight,
            packed_cache,
            long_cache,
            lengths,
            long_split,
        )
        placed = output.reshape(req_count, blocks, columns)
        result = jnp.where(is_active, placed, result)
        if phase_step < batch_count:
            incoming = shifted(output, "section", 1)
    return result.reshape(1, req_count * per_group, columns)


def solution(mesh):
    placed = (
        P(None, "req"),
        P("section", "req"),
        P("section", "req", "head", None),
        P("section", "head", None, "req"),
        P("section", "req"),
        P("section", "req", None, "head"),
        P("section", "head", "req"),
        P("section", "req", "head", None),
        P("section", None, "req", "head", None),
        P("req", None),
        P(None, "req"),
    )
    return jax.shard_map(
        local, mesh=mesh, in_specs=placed, out_specs=P("section", None, "req"), check_vma=False
    )
```

profile of v0, /device:TPU:1, one launch (start us, length us, event | category | flops | bytes accessed | tf_op | source)
XLA Modules:
  0.0 1029.1 jit_solution(9253363095233518662)
XLA Ops:
  6.7 19.1 %all-gather.10 = f32[16,1,256]{2,1,0:T(1,128)S(1)} all-gather(f32[1,1,256]{2,1,0:T(1,128)S(1)} %bitcast.379), channel_id=2, replica_groups=mesh['section'=2,'req'=16,'head'=8] {'req'}, dimensions={0}, use_global_device_ids=true | all-gather | bytes 17408 | tf_op jit(solution)/shard_map/all_gather | solution.py:19
  27.2 3.0 fusion.18
  31.0 83.1 %reduce-scatter.5.cloned.1.call-done = f32[16,1280]{1,0:T(8,128)} async-done(((f32[256,1280]{1,0:T(8,128)}), f32[16,1280]{1,0:T(8,128)}) %reduce-scatter.5.cloned.1.call-update) | async-done | bytes 81936 | tf_op jit(solution)/shard_map/reduce_scatter | solution.py:75
  115.3 16.8 %all-gather.11 = bf16[16,1,1024]{2,1,0:T(2,128)(2,1)S(1)} all-gather(bf16[1,1,1024]{2,1,0:T(2,128)(2,1)S(1)} %reshape.774), channel_id=1, replica_groups=mesh['section'=2,'req'=16,'head'=8] {'req'}, dimensions={0}, use_global_device_ids=true | all-gather | bytes 34816 | tf_op jit(solution)/shard_map/all_gather | solution.py:71
  132.2 1.7 select_reduce_fusion.3
  134.0 1.5 fusion.33
  135.6 16.4 %all-gather.12 = f32[16,2,8]{2,1,0:T(2,128)S(1)} all-gather(f32[1,2,8]{2,1,0:T(2,128)S(1)} %bitcast.371), channel_id=3, replica_groups=mesh['section'=2,'req'=16,'head'=8] {'req'}, dimensions={0}, use_global_device_ids=true | all-gather | bytes 1088 | tf_op jit(solution)/shard_map/all_gather | solution.py:19
  152.0 16.4 %all-gather.13 = f32[16,2,8]{2,1,0:T(2,128)S(1)} all-gather(f32[1,2,8]{2,1,0:T(2,128)S(1)} %bitcast.375), channel_id=4, replica_groups=mesh['section'=2,'req'=16,'head'=8] {'req'}, dimensions={0}, use_global_device_ids=true | all-gather | bytes 1088 | tf_op jit(solution)/shard_map/all_gather | solution.py:19
  168.4 16.6 %all-gather.3 = f32[32,8,128]{2,1,0:T(8,128)S(1)} all-gather(f32[2,8,128]{2,1,0:T(8,128)S(1)} %fusion.33), channel_id=5, replica_groups=mesh['section'=2,'req'=16,'head'=8] {'req'}, dimensions={0}, use_global_device_ids=true | all-gather | bytes 139264 | tf_op jit(solution)/shard_map/all_gather | solution.py:19
  185.1 1.7 while.99
  188.7 17.1 %all_gather.87 = bf16[256,1024]{1,0:T(8,128)(2,1)S(1)} all-gather(bf16[16,1024]{1,0:T(8,128)(2,1)S(1)} %bitcast.340), channel_id=1, replica_groups=mesh['section'=2,'req'=16,'head'=8] {'req'}, dimensions={0}, use_global_device_ids=true | all-gather | bytes 557056 | tf_op jit(solution)/shard_map/all_gather | solution.py:71
  205.9 1.2 fusion.30
  207.2 4.5 copy.75
  211.7 92.6 %all-reduce.5.cloned.1.call-done = f32[256,512]{1,0:T(8,128)} async-done(((f32[256,512]{1,0:T(8,128)}), f32[256,512]{1,0:T(8,128)}) %all-reduce.5.cloned.1.call-update) | async-done | bytes 524304 | tf_op jit(solution)/shard_map/psum | solution.py:84
  304.3 1.2 fusion.38
  305.6 17.8 %all-gather.14 = f32[16,1,256]{2,1,0:T(1,128)S(1)} all-gather(f32[1,1,256]{2,1,0:T(1,128)S(1)} %bitcast.378), channel_id=6, replica_groups=mesh['section'=2,'req'=16,'head'=8] {'req'}, dimensions={0}, use_global_device_ids=true | all-gather | bytes 17408 | tf_op jit(solution)/shard_map/all_gather | solution.py:19
  324.1 5.0 fusion.57
  329.2 86.3 %reduce-scatter.7.cloned.1.call-done = f32[16,3584]{1,0:T(8,128)} async-done(((f32[256,3584]{1,0:T(8,128)}), f32[16,3584]{1,0:T(8,128)}) %reduce-scatter.7.cloned.1.call-update) | async-done | bytes 229392 | tf_op jit(solution)/shard_map/reduce_scatter | solution.py:75
  416.6 19.0 %all_gather.90 = bf16[256,1792]{1,0:T(8,128)(2,1)S(1)} all-gather(bf16[16,1792]{1,0:T(8,128)(2,1)S(1)} %fusion.70), channel_id=1, replica_groups=mesh['section'=2,'req'=16,'head'=8] {'req'}, dimensions={0}, use_global_device_ids=true | all-gather | bytes 974848 | tf_op jit(solution)/shard_map/all_gather | solution.py:71
  435.5 1.4 fusion.14
  437.0 74.2 %all-reduce.7.cloned.1.call-done = f32[256,512]{1,0:T(8,128)} async-done(((f32[256,512]{1,0:T(8,128)}), f32[256,512]{1,0:T(8,128)}) %all-reduce.7.cloned.1.call-update) | async-done | bytes 524304 | tf_op jit(solution)/shard_map/psum | solution.py:84
  511.3 1.9 fusion.41
  513.2 1.3 collective-permute-start
  514.5 6.6 collective-permute-done
  521.0 1.8 fusion.42
  522.8 17.9 %all-gather.15 = f32[16,1,256]{2,1,0:T(1,128)S(1)} all-gather(f32[1,1,256]{2,1,0:T(1,128)S(1)} %bitcast.376), channel_id=7, replica_groups=mesh['section'=2,'req'=16,'head'=8] {'req'}, dimensions={0}, use_global_device_ids=true | all-gather | bytes 17408 | tf_op jit(solution)/shard_map/all_gather | solution.py:19
  541.5 2.6 fusion.16
  544.1 76.9 %reduce-scatter.9.cloned.1.call-done = f32[16,1280]{1,0:T(8,128)} async-done(((f32[256,1280]{1,0:T(8,128)}), f32[16,1280]{1,0:T(8,128)}) %reduce-scatter.9.cloned.1.call-update) | async-done | bytes 81936 | tf_op jit(solution)/shard_map/reduce_scatter | solution.py:75
  622.2 16.8 %all-gather.16 = bf16[16,1,1024]{2,1,0:T(2,128)(2,1)S(1)} all-gather(bf16[1,1,1024]{2,1,0:T(2,128)(2,1)S(1)} %reshape.784), channel_id=1, replica_groups=mesh['section'=2,'req'=16,'head'=8] {'req'}, dimensions={0}, use_global_device_ids=true | all-gather | bytes 34816 | tf_op jit(solution)/shard_map/all_gather | solution.py:71
  639.0 1.7 select_reduce_fusion.2
  640.9 1.5 fusion.32
  642.7 1.5 select_reduce_fusion
  644.4 16.4 %all-gather.17 = f32[16,2,8]{2,1,0:T(2,128)S(1)} all-gather(f32[1,2,8]{2,1,0:T(2,128)S(1)} %bitcast.370), channel_id=8, replica_groups=mesh['section'=2,'req'=16,'head'=8] {'req'}, dimensions={0}, use_global_device_ids=true | all-gather | bytes 1088 | tf_op jit(solution)/shard_map/all_gather | solution.py:19
  660.8 16.4 %all-gather.18 = f32[16,2,8]{2,1,0:T(2,128)S(1)} all-gather(f32[1,2,8]{2,1,0:T(2,128)S(1)} %bitcast.374), channel_id=9, replica_groups=mesh['section'=2,'req'=16,'head'=8] {'req'}, dimensions={0}, use_global_device_ids=true | all-gather | bytes 1088 | tf_op jit(solution)/shard_map/all_gather | solution.py:19
  677.3 16.6 %all-gather.8 = f32[32,8,128]{2,1,0:T(8,128)S(1)} all-gather(f32[2,8,128]{2,1,0:T(8,128)S(1)} %fusion.32), channel_id=10, replica_groups=mesh['section'=2,'req'=16,'head'=8] {'req'}, dimensions={0}, use_global_device_ids=true | all-gather | bytes 139264 | tf_op jit(solution)/shard_map/all_gather | solution.py:19
  693.9 1.7 while.102
  696.2 1.5 fusion.26
  697.7 17.5 %all_gather.100 = bf16[256,1024]{1,0:T(8,128)(2,1)S(1)} all-gather(bf16[16,1024]{1,0:T(8,128)(2,1)S(1)} %bitcast.341), channel_id=1, replica_groups=mesh['section'=2,'req'=16,'head'=8] {'req'}, dimensions={0}, use_global_device_ids=true | all-gather | bytes 557056 | tf_op jit(solution)/shard_map/all_gather | solution.py:71
  715.3 1.2 fusion.28
  716.6 96.9 %all-reduce.9.cloned.1.call-done = f32[256,512]{1,0:T(8,128)} async-done(((f32[256,512]{1,0:T(8,128)}), f32[256,512]{1,0:T(8,128)}) %all-reduce.9.cloned.1.call-update) | async-done | bytes 524304 | tf_op jit(solution)/shard_map/psum | solution.py:84
  813.5 1.2 fusion.46
  814.7 17.8 %all-gather.19 = f32[16,1,256]{2,1,0:T(1,128)S(1)} all-gather(f32[1,1,256]{2,1,0:T(1,128)S(1)} %bitcast.377), channel_id=11, replica_groups=mesh['section'=2,'req'=16,'head'=8] {'req'}, dimensions={0}, use_global_device_ids=true | all-gather | bytes 17408 | tf_op jit(solution)/shard_map/all_gather | solution.py:19
  833.2 5.0 fusion.54
  838.3 86.4 %reduce-scatter.11.cloned.1.call-done = f32[16,3584]{1,0:T(8,128)} async-done(((f32[256,3584]{1,0:T(8,128)}), f32[16,3584]{1,0:T(8,128)}) %reduce-scatter.11.cloned.1.call-update) | async-done | bytes 229392 | tf_op jit(solution)/shard_map/reduce_scatter | solution.py:75
  925.7 19.0 %all_gather.103 = bf16[256,1792]{1,0:T(8,128)(2,1)S(1)} all-gather(bf16[16,1792]{1,0:T(8,128)(2,1)S(1)} %fusion.69), channel_id=1, replica_groups=mesh['section'=2,'req'=16,'head'=8] {'req'}, dimensions={0}, use_global_device_ids=true | all-gather | bytes 974848 | tf_op jit(solution)/shard_map/all_gather | solution.py:71
  944.7 1.5 fusion.12
  946.2 74.3 %all-reduce.11.cloned.1.call-done = f32[256,512]{1,0:T(8,128)} async-done(((f32[256,512]{1,0:T(8,128)}), f32[256,512]{1,0:T(8,128)}) %all-reduce.11.cloned.1.call-update) | async-done | bytes 524304 | tf_op jit(solution)/shard_map/psum | solution.py:84
  1020.4 1.9 fusion.53
  (354 shorter events, 17.0 us)
Async XLA Ops:
  6.5 429.0 %copy-start = (bf16[1,1792,512]{2,1,0:T(8,128)(2,1)S(1)}, bf16[1,1792,512]{2,1,0:T(8,128)(2,1)}, u32[]{:S(2)}) copy-start(bf16[1,1792,512]{2,1,0:T(8,128)(2,1)} %param.29) | copy-start | bytes 5505028
  6.5 107.6 %reduce-scatter.5.cloned.1.call-start = ((), (), s32[]{:S(2)}) async-start(), calls=%async_computation.4 | async-start | bytes 1392640 | tf_op jit(solution)/shard_map/reduce_scatter | solution.py:75
  27.2 3.1 copy-start.9
  27.2 3.6 copy-start.10
  30.2 274.2 %all-reduce.5.cloned.1.call-start = ((), (), s32[]{:S(2)}) async-start(), calls=%async_computation.5 | async-start | bytes 1048576 | tf_op jit(solution)/shard_map/psum | solution.py:84
  30.5 156.7 %copy-start.7 = (bf16[1,2048,1,256]{3,1,2,0:T(8,128)(2,1)S(1)}, bf16[1,2048,1,256]{3,1,2,0:T(8,128)(2,1)}, u32[]{:S(2)}) copy-start(bf16[1,2048,1,256]{3,1,2,0:T(8,128)(2,1)} %param.30) | copy-start | bytes 3145732
  187.8 18.1 %copy-start.3 = (bf16[1,1,1024,512]{3,2,1,0:T(8,128)(2,1)S(1)}, bf16[1,1,1024,512]{3,2,1,0:T(8,128)(2,1)}, u32[]{:S(2)}) copy-start(bf16[1,1,1024,512]{3,2,1,0:T(8,128)(2,1)} %param.26) | copy-start | bytes 3145732
  207.1 208.4 %reduce-scatter.7.cloned.1.call-start = ((), (), s32[]{:S(2)}) async-start(), calls=%async_computation.6 | async-start | bytes 3899392 | tf_op jit(solution)/shard_map/reduce_scatter | solution.py:75
  207.2 4.5 copy-start.8
  207.2 97.1 %copy-start.2 = (bf16[256,512]{1,0:T(8,128)(2,1)S(1)}, bf16[256,512]{1,0:T(8,128)(2,1)}, u32[]{:S(2)}) copy-start(bf16[256,512]{1,0:T(8,128)(2,1)} %param.23) | copy-start | bytes 786436
  305.6 23.6 %copy-start.5 = (bf16[256,512]{1,0:T(8,128)(2,1)}, bf16[256,512]{1,0:T(8,128)(2,1)S(1)}, u32[]{:S(2)}) copy-start(bf16[256,512]{1,0:T(8,128)(2,1)S(1)} %get-tuple-element.859) | copy-start | bytes 786436
  329.2 182.1 %all-reduce.7.cloned.1.call-start = ((), (), s32[]{:S(2)}) async-start(), calls=%async_computation.7 | async-start | bytes 1048576 | tf_op jit(solution)/shard_map/psum | solution.py:84
  437.0 104.5 %copy-start.1 = (bf16[1,512,1,1280]{3,1,2,0:T(8,128)(2,1)S(1)}, bf16[1,512,1,1280]{3,1,2,0:T(8,128)(2,1)}, u32[]{:S(2)}) copy-start(bf16[1,512,1,1280]{3,1,2,0:T(8,128)(2,1)} %param.25) | copy-start | bytes 3932164
  437.0 184.0 %reduce-scatter.9.cloned.1.call-start = ((), (), s32[]{:S(2)}) async-start(), calls=%async_computation.8 | async-start | bytes 1392640 | tf_op jit(solution)/shard_map/reduce_scatter | solution.py:75
  513.2 7.9 collective-permute-start
  544.1 269.4 %all-reduce.9.cloned.1.call-start = ((), (), s32[]{:S(2)}) async-start(), calls=%async_computation.9 | async-start | bytes 1048576 | tf_op jit(solution)/shard_map/psum | solution.py:84
  695.7 19.6 %copy-start.4 = (bf16[1,1,1024,512]{3,2,1,0:T(8,128)(2,1)S(1)}, bf16[1,1,1024,512]{3,2,1,0:T(8,128)(2,1)}, u32[]{:S(2)}) copy-start(bf16[1,1,1024,512]{3,2,1,0:T(8,128)(2,1)} %param.26) | copy-start | bytes 3145732
  697.7 115.8 %copy-start.6 = (bf16[256,512]{1,0:T(8,128)(2,1)S(1)}, bf16[256,512]{1,0:T(8,128)(2,1)}, u32[]{:S(2)}) copy-start(bf16[256,512]{1,0:T(8,128)(2,1)} %get-tuple-element.857) | copy-start | bytes 786436
  716.6 208.1 %reduce-scatter.11.cloned.1.call-start = ((), (), s32[]{:S(2)}) async-start(), calls=%async_computation.10 | async-start | bytes 3899392 | tf_op jit(solution)/shard_map/reduce_scatter | solution.py:75
  838.3 182.2 %all-reduce.11.cloned.1.call-start = ((), (), s32[]{:S(2)}) async-start(), calls=%async_computation.11 | async-start | bytes 1048576 | tf_op jit(solution)/shard_map/psum | solution.py:84
Sparse Core Ops, SparseCore 0:
  30.3 83.7 reduce-scatter.4
  207.3 97.0 all-reduce.4
  329.3 86.2 reduce-scatter.6
  437.1 74.1 all-reduce.6
  544.2 76.7 reduce-scatter.8
  716.7 96.7 all-reduce.8
  838.4 86.2 reduce-scatter.10
  946.3 74.0 all-reduce.10
where the time goes:
time: 1030 us
  waiting for transfers between devices  677 us (66%)
  blocking collectives  278 us (27%)
  matrix products  31.7 us (3%)
  other arithmetic  17.4 us (2%)
  between operations  13.9 us (1%)
    psum x4, waiting for transfers between devices, head_total(): return lax.psum(values, 'head')  338 us
    reduce_scatter x4, waiting for transfers between devices, rows_project(): lax.psum_scatter(term_fn(jnp.int32(0), row_count * lax.axis_size('req')),...  333 us
    all_gather x10, blocking collectives, merged(): gathered = jax.tree.map(lambda a: lax.all_gather(a, axis), part)  171 us
    all_gather x6, blocking collectives, rows_apply(): lax.all_gather(values, 'req', axis=0, tiled=True)  106 us
  transfers between devices with their start and end apart: 9, of which 9 were waited for; matrix products, arithmetic and copies ran while one was open for 1% of the time, Pallas kernels for 0%

commit v1 on v0

v1 whole, which is shorter than its diff:
```python
import functools
import math

import jax
import jax.numpy as jnp
from jax import lax
from jax.experimental import pallas as pl
from jax.experimental.pallas import tpu as pltpu
from jax.sharding import PartitionSpec as P

HEAD = 128
LONG = 16384
EPSILON = 1e-05
NEG = -1e30
F32 = jnp.float32
BF16 = jnp.bfloat16
MESH = pl.DeviceIdType.MESH


def split_two(value, lanes):
    high = value.astype(BF16).astype(F32)
    return jnp.where(lanes < 64, high, value - high).astype(BF16)


def rope(block, table):
    swapped = jnp.concatenate([block[:, HEAD // 2 :], block[:, : HEAD // 2]], axis=1)
    return block * table[:, :HEAD] + swapped * table[:, HEAD:]


def kernel(
    dims,
    split_ref,
    tok_ref,
    gain1_ref,
    wqkv_hbm,
    wo_hbm,
    gain2_ref,
    wgu_hbm,
    wd_hbm,
    pack_hbm,
    far_hbm,
    len_ref,
    cs_ref,
    out_ref,
    wqkv,
    wo,
    wgu,
    wd,
    pack,
    far,
    xin,
    xg,
    send1,
    recv1,
    ext32,
    exts,
    csl,
    qbuf,
    score,
    att,
    lse,
    fscore,
    rows_all,
    far_all,
    send3,
    recv3,
    res_all,
    send5,
    recv5,
    hid_all,
    send7,
    recv7,
    oblk,
    out_all,
    wsem,
    s1,
    r1,
    se,
    re,
    sc,
    rc,
    s2,
    r2,
    sl,
    rl,
    s3,
    r3,
    s4,
    r4,
    s5,
    r5,
    s6,
    r6,
    s7,
    r7,
    s8,
    r8,
    su,
    ru,
    sb,
    rb,
):
    n_req, n_head, width = dims
    n_y = 4 if n_req == 16 else n_req
    n_x = n_req // n_y
    sec = lax.axis_index("section")
    me = lax.axis_index("req")
    mz = lax.axis_index("head")
    blk, cols = xin.shape[1], xin.shape[2]
    rows = n_head * blk
    slots = pack.shape[0]
    heads = 8
    qw = heads * HEAD
    ff = wd.shape[0]
    scale = 1.0 / math.sqrt(HEAD)
    half = n_req // 2

    def req_peer(k):
        x = lax.rem(lax.div(me, n_y) + lax.div(k, n_y), n_x)
        y = lax.rem(lax.rem(me, n_y) + lax.rem(k, n_y), n_y)
        return x * n_y + y

    def head_peer(k):
        return lax.rem(mz + k, n_head)

    def req_copy(src, dst, ssem, rsem, peer):
        return pltpu.make_async_remote_copy(
            src_ref=src, dst_ref=dst, send_sem=ssem, recv_sem=rsem,
            device_id={"req": peer}, device_id_type=MESH,
        )

    def head_copy(src, dst, ssem, rsem, peer):
        return pltpu.make_async_remote_copy(
            src_ref=src, dst_ref=dst, send_sem=ssem, recv_sem=rsem,
            device_id={"head": peer}, device_id_type=MESH,
        )

    def spread(copy, count, peer_of, source, target, ssem, rsem, mine):
        @pl.loop(1, count)
        def _(k):
            peer = peer_of(k)
            copy(source(peer), target.at[mine], ssem.at[k], rsem.at[mine], peer).start()

    def arrived(copy, count, peer_of, target, ssem, rsem):
        @pl.loop(1, count)
        def _(k):
            peer = peer_of(k)
            copy(target.at[peer], target.at[peer], ssem.at[k], rsem.at[peer], peer).wait_recv()

    def sent(copy, count, peer_of, source, target, ssem, rsem, mine):
        @pl.loop(1, count)
        def _(k):
            peer = peer_of(k)
            copy(source(peer), target.at[mine], ssem.at[k], rsem.at[mine], peer).wait_send()

    loads = [
        pltpu.make_async_copy(src, dst, wsem.at[n])
        for n, (src, dst) in enumerate(
            ((wqkv_hbm, wqkv), (pack_hbm, pack), (far_hbm, far), (wo_hbm, wo), (wgu_hbm, wgu), (wd_hbm, wd))
        )
    ]
    for load in loads:
        load.start()

    barrier = pltpu.get_barrier_semaphore()

    @pl.loop(1, n_req)
    def _(k):
        pl.semaphore_signal(barrier, inc=1, device_id={"req": req_peer(k)}, device_id_type=MESH)

    @pl.loop(1, n_head)
    def _(k):
        pl.semaphore_signal(barrier, inc=1, device_id={"head": head_peer(k)}, device_id_type=MESH)

    @pl.loop(0, n_head)
    def _(k):
        pl.semaphore_signal(
            barrier, inc=1, device_id={"section": 1 - sec, "head": head_peer(k)}, device_id_type=MESH
        )

    pl.semaphore_wait(barrier, n_req - 1 + n_head - 1 + n_head)

    for j in range(2):
        owner = j * half

        @pl.when(me == owner)
        def _(j=j):
            csl[j] = cs_ref[0:8, :]

            @pl.loop(1, n_req)
            def _(k):
                peer = req_peer(k)
                req_copy(csl.at[j], csl.at[j], sc.at[j, k], rc.at[j], peer).start()

    @pl.when(sec == 0)
    def _():
        xin[...] = tok_ref[...]

    @pl.when(sec == 1)
    def _():
        @pl.loop(0, n_head)
        def _(k):
            pltpu.make_async_remote_copy(
                src_ref=xin.at[k], dst_ref=xin.at[k], send_sem=su.at[k], recv_sem=ru.at[k],
                device_id={"section": 0, "head": k}, device_id_type=MESH,
            ).wait_recv()

        pltpu.make_async_remote_copy(
            src_ref=xin, dst_ref=out_all, send_sem=sb.at[0], recv_sem=rb.at[0],
            device_id={"section": 0}, device_id_type=MESH,
        ).start()

    lanes128 = lax.broadcasted_iota(jnp.int32, (rows, HEAD), 1)

    x = xin[...].reshape(rows, cols).astype(F32)
    squares = jnp.sum(x * x, axis=1, keepdims=True)
    xg[...] = (x * gain1_ref[...].astype(F32)).astype(BF16)
    pair = split_two(squares, lanes128)
    send1[:, :, qw + 2 * HEAD :] = pair.reshape(n_req, 16, HEAD)
    loads[0].wait()

    @pl.loop(0, (qw + 2 * HEAD) // 256)
    def _(c):
        at = pl.ds(pl.multiple_of(c * 256, 256), 256)
        part = jnp.dot(xg[...], wqkv[:, at], preferred_element_type=F32)
        send1[:, :, at] = part.astype(BF16).reshape(n_req, 16, 256)

    spread(req_copy, n_req, req_peer, lambda p: send1.at[p], recv1, s1, r1, me)

    for j in range(2):
        row = send1[j * half].astype(F32)[0:1]
        for h in range(heads):
            ext32[j * 8 + h : j * 8 + h + 1, 0:HEAD] = row[:, h * HEAD : (h + 1) * HEAD]
        ext32[j * 8 : j * 8 + 8, HEAD:] = jnp.broadcast_to(row[:, qw + 2 * HEAD :], (8, HEAD))
    exts[me] = ext32[...].astype(BF16)
    spread(req_copy, n_req, req_peer, lambda p: exts.at[me], exts, se, re, me)
    recv1[me] = send1[me]

    r_id = lax.broadcasted_iota(jnp.int32, (16 * heads, 16), 0) & 15
    k_id = lax.broadcasted_iota(jnp.int32, (16 * heads, 16), 1)
    lens = jnp.broadcast_to(len_ref[...].astype(F32), (16 * heads, 16))
    seg_end = jnp.sum(jnp.where(k_id <= r_id, lens, 0.0), axis=1, keepdims=True).astype(jnp.int32)
    seg_start = jnp.sum(jnp.where(k_id < r_id, lens, 0.0), axis=1, keepdims=True).astype(jnp.int32)

    for j in range(2):

        @pl.when(me != j * half)
        def _(j=j):
            req_copy(csl.at[j], csl.at[j], sc.at[j, 1], rc.at[j], me).wait_recv()

    arrived(req_copy, n_req, req_peer, exts, se, re)
    total = exts[0].astype(F32)
    for p in range(1, n_req):
        total = total + exts[p].astype(F32)
    far_scale = lax.rsqrt((total[:, HEAD : HEAD + 1] + total[:, HEAD + 64 : HEAD + 65]) / width + EPSILON)
    table = jnp.concatenate(
        [jnp.broadcast_to(csl[0][0:1], (8, 2 * HEAD)), jnp.broadcast_to(csl[1][0:1], (8, 2 * HEAD))], axis=0
    )
    far_query = rope(total[:, :HEAD] * far_scale, table).astype(BF16)
    loads[1].wait()
    loads[2].wait()
    chunk = min(512, slots)
    n_chunk = slots // chunk
    contract = (((1,), (1,)), ((), ()))
    low_half = lax.broadcasted_iota(jnp.int32, (16, chunk), 0) < 8
    live = jnp.where(low_half, split_ref[0, 0], split_ref[1, 0])

    def far_first(c, best):
        at = pl.ds(pl.multiple_of(c * chunk, chunk), chunk)
        a = lax.dot_general(far_query, far[0, at, 0:HEAD], contract, preferred_element_type=F32)
        b = lax.dot_general(far_query, far[1, at, 0:HEAD], contract, preferred_element_type=F32)
        slot = lax.broadcasted_iota(jnp.int32, (16, chunk), 1) + c * chunk
        value = jnp.where(slot < live, jnp.where(low_half, a, b) * scale, NEG)
        fscore[:, at] = value
        return jnp.maximum(best, jnp.max(value, axis=1, keepdims=True))

    far_max = lax.fori_loop(0, n_chunk, far_first, jnp.full((16, 1), NEG, F32))
    low_rows = lax.broadcasted_iota(jnp.int32, (16, HEAD), 0) < 8

    def far_second(c, carry):
        totals, summed = carry
        at = pl.ds(pl.multiple_of(c * chunk, chunk), chunk)
        w = jnp.exp(fscore[:, at] - far_max).astype(BF16)
        a = jnp.dot(w, far[0, at, HEAD:], preferred_element_type=F32)
        b = jnp.dot(w, far[1, at, HEAD:], preferred_element_type=F32)
        totals = totals + jnp.sum(w.astype(F32), axis=1, keepdims=True)
        return totals, summed + jnp.where(low_rows, a, b)

    far_totals, far_sum = lax.fori_loop(
        0, n_chunk, far_second, (jnp.zeros((16, 1), F32), jnp.zeros((16, HEAD), F32))
    )
    far_out = far_sum / far_totals
    far_lse = jnp.broadcast_to(far_max + jnp.log(far_totals), (16, HEAD))

    arrived(req_copy, n_req, req_peer, recv1, s1, r1)

    def total_of(ref, at):
        value = ref[0, :, at].astype(F32)
        for p in range(1, ref.shape[0]):
            value = value + ref[p, :, at].astype(F32)
        return value

    stat = total_of(recv1, pl.ds(qw + 2 * HEAD, HEAD))
    row_scale = lax.rsqrt((stat[:, 0:1] + stat[:, 64:65]) / width + EPSILON)
    cs = cs_ref[...]

    @pl.loop(0, heads)
    def _(h):
        at = pl.ds(pl.multiple_of(h * HEAD, HEAD), HEAD)
        qbuf[h] = rope(total_of(recv1, at) * row_scale, cs).astype(BF16)

    new_key = rope(total_of(recv1, pl.ds(qw, HEAD)) * row_scale, cs).astype(BF16)
    new_value = (total_of(recv1, pl.ds(qw + HEAD, HEAD)) * row_scale).astype(BF16)
    queries = qbuf[...].reshape(heads * 16, HEAD)
    keys = jnp.concatenate([new_key.astype(F32)] * heads, axis=0)
    values = jnp.concatenate([new_value.astype(F32)] * heads, axis=0)
    own = jnp.sum(queries.astype(F32) * keys, axis=1, keepdims=True) * scale

    def near_first(c, best):
        at = pl.ds(pl.multiple_of(c * chunk, chunk), chunk)
        s = lax.dot_general(queries, pack[at, 0:HEAD], contract, preferred_element_type=F32)
        slot = lax.broadcasted_iota(jnp.int32, (heads * 16, chunk), 1) + c * chunk
        value = jnp.where((slot >= seg_start) & (slot < seg_end), s * scale, NEG)
        score[:, at] = value
        return jnp.maximum(best, jnp.max(value, axis=1, keepdims=True))

    row_max = lax.fori_loop(0, n_chunk, near_first, own)
    own_weight = jnp.exp(own - row_max).astype(BF16).astype(F32)

    def near_second(c, carry):
        totals, summed = carry
        at = pl.ds(pl.multiple_of(c * chunk, chunk), chunk)
        w = jnp.exp(score[:, at] - row_max).astype(BF16)
        summed = summed + jnp.dot(w, pack[at, HEAD:], preferred_element_type=F32)
        return totals + jnp.sum(w.astype(F32), axis=1, keepdims=True), summed

    totals, summed = lax.fori_loop(0, n_chunk, near_second, (own_weight, own_weight * values))
    attended = summed / totals
    att[...] = attended
    lse[...] = jnp.broadcast_to(row_max + jnp.log(totals), (heads * 16, HEAD))
    for h in range(heads):
        rows_all[me, :, h * HEAD : (h + 1) * HEAD] = attended[h * 16 : (h + 1) * 16].astype(BF16)
    spread(req_copy, n_req, req_peer, lambda p: rows_all.at[me], rows_all, s2, r2, me)

    first_out = att[pl.ds(0, heads, stride=16), :]
    first_lse = lse[pl.ds(0, heads, stride=16), :]
    near_out = jnp.concatenate([first_out, first_out], axis=0)
    near_lse = jnp.concatenate([first_lse, first_lse], axis=0)
    which = lax.broadcasted_iota(jnp.int32, (16, HEAD), 0)
    owned = jnp.where(which < 8, 0, half) == me
    peak = jnp.maximum(far_lse, near_lse)
    fa = jnp.exp(far_lse - peak)
    na = jnp.exp(near_lse - peak)
    both_out = (fa * far_out + na * near_out) / (fa + na)
    part_out = jnp.where(owned, both_out, far_out)
    part_lse = jnp.where(owned, peak + jnp.log(fa + na), far_lse)
    lane = lax.broadcasted_iota(jnp.int32, (16, HEAD), 1)
    high = part_lse.astype(BF16).astype(F32)
    middle = (part_lse - high).astype(BF16).astype(F32)
    low = part_lse - high - middle
    far_all[me, :, 0:HEAD] = part_out.astype(BF16)
    far_all[me, :, HEAD:] = jnp.where(lane < 32, high, jnp.where(lane < 64, middle, low)).astype(BF16)
    spread(req_copy, n_req, req_peer, lambda p: far_all.at[me], far_all, sl, rl, me)

    arrived(req_copy, n_req, req_peer, far_all, sl, rl)
    parts = []
    for p in range(n_req):
        part = far_all[p].astype(F32)
        parts.append(part[:, HEAD : HEAD + 1] + part[:, HEAD + 32 : HEAD + 33] + part[:, HEAD + 64 : HEAD + 65])
    peak = functools.reduce(jnp.maximum, parts)
    den = jnp.zeros((16, 1), F32)
    num = jnp.zeros((16, HEAD), F32)
    for p in range(n_req):
        w = jnp.exp(parts[p] - peak)
        den = den + w
        num = num + w * far_all[p, :, 0:HEAD].astype(F32)
    long_out = num / den
    arrived(req_copy, n_req, req_peer, rows_all, s2, r2)
    first = lax.broadcasted_iota(jnp.int32, (16, qw), 0) == 0
    for j in range(2):
        flat = jnp.concatenate([long_out[j * 8 + h : j * 8 + h + 1] for h in range(heads)], axis=1)
        block = rows_all[j * half].astype(F32)
        rows_mixed = jnp.where(first, jnp.broadcast_to(flat, (16, qw)), block).astype(BF16)
        xg_rows = rows_mixed
        if j == 0:
            mixed0 = xg_rows
        else:
            mixed1 = xg_rows

    loads[3].wait()
    send_rows = [mixed0 if g == 0 else mixed1 if g == half else rows_all[g] for g in range(n_req)]
    lhs = jnp.concatenate(send_rows, axis=0)

    n_tile = min(256, cols)

    for c in range(cols // n_tile):
        at = pl.ds(c * n_tile, n_tile)
        part = jnp.dot(lhs, wo[:, at], preferred_element_type=F32)
        send3[:, :, at] = part.astype(BF16).reshape(n_head, blk, n_tile)

    spread(head_copy, n_head, head_peer, lambda p: send3.at[p], recv3, s3, r3, mz)
    recv3[mz] = send3[mz]
    arrived(head_copy, n_head, head_peer, recv3, s3, r3)
    residual = xin[mz].astype(F32) + total_of(recv3, pl.ds(0, cols))
    res_all[mz] = residual.astype(BF16)
    spread(head_copy, n_head, head_peer, lambda p: res_all.at[mz], res_all, s4, r4, mz)
    arrived(head_copy, n_head, head_peer, res_all, s4, r4)

    x = res_all[...].reshape(rows, cols).astype(F32)
    squares = jnp.sum(x * x, axis=1, keepdims=True)
    xg[...] = (x * gain2_ref[...].astype(F32)).astype(BF16)
    pair = split_two(squares, lanes128)
    send5[:, :, 2 * ff :] = pair.reshape(n_req, 16, HEAD)
    loads[4].wait()

    @pl.loop(0, 2 * ff // 256)
    def _(c):
        at = pl.ds(pl.multiple_of(c * 256, 256), 256)
        part = jnp.dot(xg[...], wgu[:, at], preferred_element_type=F32)
        send5[:, :, at] = part.astype(BF16).reshape(n_req, 16, 256)

    spread(req_copy, n_req, req_peer, lambda p: send5.at[p], recv5, s5, r5, me)
    recv5[me] = send5[me]
    arrived(req_copy, n_req, req_peer, recv5, s5, r5)
    stat = total_of(recv5, pl.ds(2 * ff, HEAD))
    row_scale = lax.rsqrt((stat[:, 0:1] + stat[:, 64:65]) / width + EPSILON)

    @pl.loop(0, ff // 256)
    def _(c):
        at = pl.ds(pl.multiple_of(c * 256, 256), 256)
        up_at = pl.ds(pl.multiple_of(ff + c * 256, 256), 256)
        gate = total_of(recv5, at) * row_scale
        up = total_of(recv5, up_at) * row_scale
        hid_all[me, :, at] = (gate / (1.0 + jnp.exp(-gate)) * up).astype(BF16)

    spread(req_copy, n_req, req_peer, lambda p: hid_all.at[me], hid_all, s6, r6, me)
    arrived(req_copy, n_req, req_peer, hid_all, s6, r6)

    loads[5].wait()

    @pl.loop(0, cols // n_tile)
    def _(c):
        at = pl.ds(pl.multiple_of(c * n_tile, n_tile), n_tile)
        part = jnp.dot(hid_all[...].reshape(rows, ff), wd[:, at], preferred_element_type=F32)
        send7[:, :, at] = part.astype(BF16).reshape(n_head, blk, n_tile)

    spread(head_copy, n_head, head_peer, lambda p: send7.at[p], recv7, s7, r7, mz)
    recv7[mz] = send7[mz]
    arrived(head_copy, n_head, head_peer, recv7, s7, r7)
    oblk[...] = (res_all[mz].astype(F32) + total_of(recv7, pl.ds(0, cols))).astype(BF16)

    def hand_over(k):
        peer = head_peer(k)
        return pltpu.make_async_remote_copy(
            src_ref=oblk, dst_ref=xin.at[mz], send_sem=su.at[k], recv_sem=ru.at[mz],
            device_id={"section": 1, "head": peer}, device_id_type=MESH,
        )

    @pl.when(sec == 0)
    def _():
        @pl.loop(0, n_head)
        def _(k):
            hand_over(k).start()

        pltpu.make_async_remote_copy(
            src_ref=xin, dst_ref=out_all, send_sem=sb.at[0], recv_sem=rb.at[0],
            device_id={"section": 1}, device_id_type=MESH,
        ).wait_recv()

        @pl.loop(0, n_head)
        def _(k):
            hand_over(k).wait_send()

    @pl.when(sec == 1)
    def _():
        out_all[mz] = oblk[...]
        spread(head_copy, n_head, head_peer, lambda p: oblk, out_all, s8, r8, mz)
        arrived(head_copy, n_head, head_peer, out_all, s8, r8)
        sent(head_copy, n_head, head_peer, lambda p: oblk, out_all, s8, r8, mz)
        pltpu.make_async_remote_copy(
            src_ref=xin, dst_ref=out_all, send_sem=sb.at[0], recv_sem=rb.at[0],
            device_id={"section": 0}, device_id_type=MESH,
        ).wait_send()

    out_ref[...] = out_all[...]

    for j in range(2):

        @pl.when(me == j * half)
        def _(j=j):
            @pl.loop(1, n_req)
            def _(k):
                peer = req_peer(k)
                req_copy(csl.at[j], csl.at[j], sc.at[j, k], rc.at[j], peer).wait_send()

    sent(req_copy, n_req, req_peer, lambda p: send1.at[p], recv1, s1, r1, me)
    sent(req_copy, n_req, req_peer, lambda p: exts.at[me], exts, se, re, me)
    sent(req_copy, n_req, req_peer, lambda p: rows_all.at[me], rows_all, s2, r2, me)
    sent(req_copy, n_req, req_peer, lambda p: far_all.at[me], far_all, sl, rl, me)
    sent(head_copy, n_head, head_peer, lambda p: send3.at[p], recv3, s3, r3, mz)
    sent(head_copy, n_head, head_peer, lambda p: res_all.at[mz], res_all, s4, r4, mz)
    sent(req_copy, n_req, req_peer, lambda p: send5.at[p], recv5, s5, r5, me)
    sent(req_copy, n_req, req_peer, lambda p: hid_all.at[me], hid_all, s6, r6, me)
    sent(head_copy, n_head, head_peer, lambda p: send7.at[p], recv7, s7, r7, mz)


def rope_table(position):
    half = HEAD // 2
    freq_ids = jnp.arange(half).astype(F32)
    inverse = 1.0 / 10000.0 ** (freq_ids * 2.0 / HEAD)
    angles = position.astype(F32)[:, None] * inverse[None, :]
    cosine, sine = jnp.cos(angles), jnp.sin(angles)
    return jnp.concatenate([cosine, cosine, -sine, sine], axis=-1)


def local(
    tokens,
    attention_gain,
    query_key_value_weight,
    head_output_weight,
    feedforward_gain,
    gate_up,
    down_weight,
    packed_cache,
    long_cache,
    lengths,
    long_split,
):
    n_req = lax.axis_size("req")
    n_head = lax.axis_size("head")
    group = lax.axis_index("req")
    rows, cols = tokens.shape
    blk = rows // n_head
    qkv = query_key_value_weight.shape[3]
    qw = head_output_weight.shape[2]
    ff = down_weight.shape[1]
    slots = packed_cache.shape[1]
    far_slots = long_cache.shape[2]
    assert slots == far_slots and rows == n_req * 16
    is_long = (jnp.arange(16) == 0) & ((group == 0) | (group == n_req // 2))
    table = rope_table(lengths[0] + jnp.where(is_long, LONG, 0).astype(jnp.int32))
    vmem = pl.BlockSpec(memory_space=pltpu.VMEM)
    hbm = pl.BlockSpec(memory_space=pl.ANY)
    smem = pl.BlockSpec(memory_space=pltpu.SMEM)

    def dma(*shape):
        return pltpu.SemaphoreType.DMA(shape)

    out = pl.pallas_call(
        functools.partial(kernel, (n_req, n_head, cols * n_req)),
        out_shape=jax.ShapeDtypeStruct((n_head, blk, cols), BF16),
        in_specs=[smem, vmem, vmem, hbm, hbm, vmem, hbm, hbm, hbm, hbm, vmem, vmem],
        out_specs=vmem,
        scratch_shapes=[
            pltpu.VMEM((cols, qkv), BF16),
            pltpu.VMEM((qw, cols), BF16),
            pltpu.VMEM((cols, 2 * ff), BF16),
            pltpu.VMEM((ff, cols), BF16),
            pltpu.VMEM((slots, 2 * HEAD), BF16),
            pltpu.VMEM((2, far_slots, 2 * HEAD), BF16),
            pltpu.VMEM((n_head, blk, cols), BF16),
            pltpu.VMEM((rows, cols), BF16),
            pltpu.VMEM((n_req, 16, qkv + HEAD), BF16),
            pltpu.VMEM((n_req, 16, qkv + HEAD), BF16),
            pltpu.VMEM((16, 2 * HEAD), F32),
            pltpu.VMEM((n_req, 16, 2 * HEAD), BF16),
            pltpu.VMEM((2, 8, 2 * HEAD), F32),
            pltpu.VMEM((8, 16, HEAD), BF16),
            pltpu.VMEM((128, slots), F32),
            pltpu.VMEM((128, HEAD), F32),
            pltpu.VMEM((128, HEAD), F32),
            pltpu.VMEM((16, far_slots), F32),
            pltpu.VMEM((n_req, 16, qw), BF16),
            pltpu.VMEM((n_req, 16, 2 * HEAD), BF16),
            pltpu.VMEM((n_head, blk, cols), BF16),
            pltpu.VMEM((n_head, blk, cols), BF16),
            pltpu.VMEM((n_head, blk, cols), BF16),
            pltpu.VMEM((n_req, 16, 2 * ff + HEAD), BF16),
            pltpu.VMEM((n_req, 16, 2 * ff + HEAD), BF16),
            pltpu.VMEM((n_req, 16, ff), BF16),
            pltpu.VMEM((n_head, blk, cols), BF16),
            pltpu.VMEM((n_head, blk, cols), BF16),
            pltpu.VMEM((blk, cols), BF16),
            pltpu.VMEM((n_head, blk, cols), BF16),
            dma(6),
            dma(n_req), dma(n_req),
            dma(n_req), dma(n_req),
            dma(2, n_req), dma(2),
            dma(n_req), dma(n_req),
            dma(n_req), dma(n_req),
            dma(n_head), dma(n_head),
            dma(n_head), dma(n_head),
            dma(n_req), dma(n_req),
            dma(n_req), dma(n_req),
            dma(n_head), dma(n_head),
            dma(n_head), dma(n_head),
            dma(n_head), dma(n_head),
            dma(1), dma(1),
        ],
        compiler_params=pltpu.CompilerParams(
            collective_id=0, has_side_effects=True, vmem_limit_bytes=56 * 2**20
        ),
    )(
        long_split,
        tokens.reshape(n_head, blk, cols),
        attention_gain,
        query_key_value_weight.reshape(cols, qkv),
        head_output_weight.reshape(qw, cols),
        feedforward_gain,
        gate_up.reshape(cols, 2 * ff),
        down_weight.reshape(ff, cols),
        packed_cache.reshape(slots, 2 * HEAD),
        long_cache.reshape(2, far_slots, 2 * HEAD),
        lengths,
        table,
    )
    return out.reshape(1, rows, cols)


def solution(mesh):
    placed = (
        P(None, "req"),
        P("section", "req"),
        P("section", "req", "head", None),
        P("section", "head", None, "req"),
        P("section", "req"),
        P("section", "req", None, "head"),
        P("section", "head", "req"),
        P("section", "req", "head", None),
        P("section", None, "req", "head", None),
        P("req", None),
        P(None, "req"),
    )
    return jax.shard_map(
        local, mesh=mesh, in_specs=placed, out_specs=P("section", None, "req"), check_vma=False
    )
```

time: 1030 us -> 187 us (0.18)
  waiting for transfers between devices: 677 us -> 0 us
  blocking collectives: 278 us -> 0 us
  Pallas kernels: 0 us -> 178 us
  matrix products: 31.7 us -> 0 us
  other arithmetic: 17.4 us -> 1.47 us
  between operations: 13.9 us -> 0.02 us
    psum x4 -> x0, waiting for transfers between devices: 338 us -> none  [head_total(): return lax.psum(values, 'head')]
    reduce_scatter x4 -> x0, waiting for transfers between devices: 333 us -> none  [rows_project(): lax.psum_scatter(term_fn(jnp.int32(0), row_count * lax.axis_size('req')),...]
    all_gather x16 -> x0, blocking collectives: 278 us -> none  [the longest x10 171 us: merged(): gathered = jax.tree.map(lambda a: lax.all_gather(a, axis), part)]
    pallas_call x0 -> x1, Pallas kernels: none -> 178 us  [local(): pl.pallas_call(functools.partial(kernel, (n_req, n_head, cols * n_req)),...]
    dot_general x18 -> x0, matrix products: 31.7 us -> none  [the longest x2 10.1 us: ff_term(): return jnp.dot(normed_two, ff_weights, preferred_element_type=jnp.float32)]
  transfers between devices with their start and end apart: 9 -> 0, of which waited for: 9 -> 0; matrix products, arithmetic and copies ran while one was open for 1% -> 0% of each run, Pallas kernels for 0% -> 0%
where the time goes in v1:
time: 187 us
  Pallas kernels  178 us (95%)
  local copies, waits for them, and re-layouts  7.38 us (4%)
    pallas_call x1, Pallas kernels, local(): pl.pallas_call(functools.partial(kernel, (n_req, n_head, cols * n_req)),...  178 us
    unnamed x3, local copies, waits for them, and re-layouts  7.38 us

profile of v1, /device:TPU:1, one launch (start us, length us, event | category | flops | bytes accessed | tf_op | source)
XLA Modules:
  0.0 186.8 jit_solution(16052389573813565255)
XLA Ops:
  0.0 0.7 fusion.2
  0.7 1.3 copy.12.split_ref
  2.0 0.1 multiply_cosine_fusion
  2.1 0.7 pad_maximum_fusion.cs_ref
  2.8 4.4 %copy.13 = bf16[64,8,2,1792]{3,1,2,0:T(8,128)(2,1)} copy(bf16[64,8,2,1792]{3,2,1,0:T(2,128)(2,1)} %bitcast.15) | data formatting | bytes 7340032
  7.2 177.9 %shard_map.109 = bf16[8,32,512]{2,1,0:T(8,128)(2,1)} custom-call(s32[2,1]{1,0:T(2,128)} %copy.12.split_ref, bf16[8,32,512]{2,1,0:T(8,128)(2,1)} %bitcast.22, bf16[1,512]{1,0:T(2,128)(2,1)} %gain1_ref.1, bf16[512,1280]{1,0:T(8,128)(2,1)} %bitcast.18, bf16[1024,512]{1,0:T(8,128)(2,1)} %bitcast.19, bf16[1,512]{1,0:T(2,128)(2,1)} %gain2_ref.1, ...), custom_call_target="tpu_custom_call" | custom-call | tf_op jit(solution)/shard_map/pallas_call | solution.py:549
  185.1 1.7 copy.15
  (1 shorter events, 0.0 us)

commit v2 on v0

v2 whole, which is shorter than its diff:
```python
import functools
import math

import jax
import jax.numpy as jnp
import numpy as np
from jax import lax
from jax.experimental import pallas as pl
from jax.experimental.pallas import tpu as pltpu
from jax.sharding import PartitionSpec as P

HEAD = 128
HEADS = 8
LONG = 16384
EPSILON = 1e-05
NEG = -1e30
F32 = jnp.float32
BF16 = jnp.bfloat16
MESH = pl.DeviceIdType.MESH
SIDE = 4


def split_two(value, lanes):
    high = value.astype(BF16).astype(F32)
    return jnp.where(lanes < 64, high, value - high).astype(BF16)


def rope(block, table):
    swapped = jnp.concatenate([block[:, HEAD // 2 :], block[:, : HEAD // 2]], axis=1)
    return block * table[0] + swapped * table[1]


def rope_tables(position, inverse):
    angles = position * inverse
    lane = lax.broadcasted_iota(jnp.int32, angles.shape, 1)
    sine = jnp.sin(angles)
    return jnp.cos(angles), jnp.where(lane < HEAD // 2, -sine, sine)


def kernel(dims, ff_parts, split_ref, tok_hbm, gain1_ref, wqkv_hbm, wo_hbm, gain2_ref, raw_hbm, wd_hbm, pack_hbm, far_hbm,
           len_ref, inv_ref, out_ref, scratch):
    n_req, n_head, width = dims
    s = scratch
    sec = lax.axis_index("section")
    me = lax.axis_index("req")
    mz = lax.axis_index("head")
    mx, my = lax.div(me, SIDE), lax.rem(me, SIDE)
    xin = s["xin"]
    n_half, _, blk, hcols = xin.shape
    cols = n_half * hcols
    rows = n_head * blk
    slots = s["pack"].shape[0]
    qw = HEADS * HEAD
    ff = s["wd"].shape[0]
    scale = 1.0 / math.sqrt(HEAD)
    mid = n_req // 2
    stat_at = qw + 2 * HEAD
    ext_at = stat_at + HEAD

    def remote(source, target, name, where, peer):
        return pltpu.make_async_remote_copy(
            src_ref=source, dst_ref=target, send_sem=s["ss_" + name].at[where], recv_sem=s["rs_" + name].at[where],
            device_id=peer, device_id_type=MESH,
        )

    def req_peer(k):
        return {"req": lax.rem(mx + lax.div(k, SIDE), SIDE) * SIDE + lax.rem(my + lax.rem(k, SIDE), SIDE)}

    def head_peer(k):
        return {"head": lax.rem(mz + k, n_head)}

    def spread_req(name, source, target, where=0):
        @pl.loop(1, n_req)
        def _(k):
            peer = req_peer(k)
            remote(source(peer["req"]), target.at[me], name, where, peer).start()

    def spread_head(name, source, target, where=0):
        @pl.loop(1, n_head)
        def _(k):
            peer = head_peer(k)
            remote(source(peer["head"]), target.at[mz], name, where, peer).start()

    def arrived(name, target, count, where=0):
        whole = target.at[pl.ds(0, count)]
        remote(whole, whole, name, where, {"section": 1 - sec}).wait_recv()

    def sent(name, source, count, where=0):
        whole = source.at[pl.ds(0, count)]
        remote(whole, whole, name, where, {"section": 1 - sec}).wait_send()

    def load(source, target, n):
        return pltpu.make_async_copy(source, target, s["wsem"].at[n])

    load_qkv = load(wqkv_hbm, s["wqkv"], 0)
    load_raw = load(raw_hbm, s["raw"], 1)
    load_pack = load(pack_hbm, s["pack"], 2)
    load_far = load(far_hbm, s["far"], 3)
    load_wo = load(wo_hbm, s["wo"], 4)
    load_wd = load(wd_hbm, s["wd"], 5)
    load_qkv.start()

    @pl.when(sec == 0)
    def _():
        for h in range(n_half):
            load(tok_hbm.at[:, :, pl.ds(h * hcols, hcols)], xin.at[h], 6 + h).start()

    barrier = pltpu.get_barrier_semaphore()

    @pl.loop(1, n_req)
    def _(k):
        pl.semaphore_signal(barrier, inc=1, device_id=req_peer(k), device_id_type=MESH)

    @pl.loop(1, n_head)
    def _(k):
        pl.semaphore_signal(barrier, inc=1, device_id=head_peer(k), device_id_type=MESH)

    @pl.loop(0, n_head)
    def _(k):
        pl.semaphore_signal(barrier, inc=1, device_id={"section": 1 - sec, **head_peer(k)}, device_id_type=MESH)

    for other in (load_raw, load_pack, load_far, load_wo, load_wd):
        other.start()

    def lane_sum(mask, shape):
        lens = jnp.broadcast_to(len_ref[...].astype(F32), shape)
        return jnp.sum(jnp.where(mask, lens, 0.0), axis=1, keepdims=True)

    r16 = lax.broadcasted_iota(jnp.int32, (16, 16), 0)
    k16 = lax.broadcasted_iota(jnp.int32, (16, 16), 1)
    is_long = (lax.broadcasted_iota(jnp.int32, (16, 1), 0) == 0) & ((me == 0) | (me == mid))
    position = lane_sum(k16 == r16, (16, 16)) + jnp.where(is_long, float(LONG), 0.0)

    lanes = lax.broadcasted_iota(jnp.int32, (rows, HEAD), 1)
    lane16 = lax.broadcasted_iota(jnp.int32, (16, HEAD), 1)

    def normed(source, gain_ref):
        squares = jnp.zeros((rows, 1), F32)
        for h in range(n_half):
            at = pl.ds(h * hcols, hcols)
            x = source[h].reshape(rows, hcols).astype(F32)
            squares = squares + jnp.sum(x * x, axis=1, keepdims=True)
            s["xg"][:, at] = (x * gain_ref[:, at].astype(F32)).astype(BF16)
        return squares

    def first_products():
        squares = normed(xin, gain1_ref)
        s["send1"][:, :, stat_at : stat_at + HEAD] = split_two(squares, lanes).reshape(n_req, 16, HEAD)
        load_qkv.wait()

        @pl.loop(0, stat_at // 256)
        def _(c):
            at = pl.ds(pl.multiple_of(c * 256, 256), 256)
            part = jnp.dot(s["xg"][...], s["wqkv"][:, at], preferred_element_type=F32)
            s["send1"][:, :, at] = part.astype(BF16).reshape(n_req, 16, 256)

        ext = s["ext"]
        for j in range(2):
            row = s["send1"][j * mid].astype(F32)[0:1]
            for h in range(HEADS):
                ext[j * 8 + h : j * 8 + h + 1, 0:HEAD] = row[:, h * HEAD : (h + 1) * HEAD]
            ext[j * 8 : j * 8 + 8, HEAD:] = jnp.broadcast_to(row[:, stat_at : stat_at + HEAD], (8, HEAD))
        first = position[0:1]
        upper = jnp.floor(first * (1.0 / 256.0))
        lower = first - 256.0 * upper
        tail = ext[:, HEAD:]
        stats = jnp.where(lane16 < 32, tail[:, 0:1], tail[:, 64:65])
        places = jnp.where(lane16 < 96, upper, lower)
        tail = jnp.where(lane16 < 64, stats, places).astype(BF16)
        head = ext[:, 0:HEAD].astype(BF16)
        for g in range(n_req):
            s["send1"][g, :, ext_at : ext_at + HEAD] = head
            s["send1"][g, :, ext_at + HEAD :] = tail

    def split_gate():
        load_raw.wait()
        raw, wgu = s["raw"], s["wgu"]

        @pl.loop(0, cols // 16)
        def _(k):
            at = pl.ds(pl.multiple_of(k * 16, 16), 16)
            for c in range(ff // HEAD):
                source = pl.ds(c * HEAD, HEAD)
                wgu[at, pl.ds(c * 256, HEAD)] = raw[at, 0, source]
                wgu[at, pl.ds(c * 256 + HEAD, HEAD)] = raw[at, 1, source]

    @pl.when(sec == 0)
    def _():
        for h in range(n_half):
            load(tok_hbm.at[:, :, pl.ds(h * hcols, hcols)], xin.at[h], 6 + h).wait()
        first_products()

    pl.semaphore_wait(barrier, n_req - 1 + n_head - 1 + n_head)

    @pl.when(sec == 1)
    def _():
        split_gate()
        for h in range(n_half):
            remote(xin.at[h], xin.at[h], "in", h, {"section": 0}).wait_recv()
        remote(xin, s["out"], "back", 0, {"section": 0}).start()
        first_products()

    spread_req("p1", lambda p: s["send1"].at[p], s["recv1"])
    s["recv1"][me] = s["send1"][me]

    @pl.when(sec == 0)
    def _():
        split_gate()

    own_table = rope_tables(position, inv_ref[...])
    r_id = lax.broadcasted_iota(jnp.int32, (16 * HEADS, 16), 0) & 15
    k_id = lax.broadcasted_iota(jnp.int32, (16 * HEADS, 16), 1)
    seg_end = lane_sum(k_id <= r_id, (16 * HEADS, 16)).astype(jnp.int32)
    seg_start = lane_sum(k_id < r_id, (16 * HEADS, 16)).astype(jnp.int32)
    load_pack.wait()
    load_far.wait()
    pack, far = s["pack"], s["far"]
    recv1 = s["recv1"]
    arrived("p1", recv1, n_req - 1)

    def total_of(ref, at):
        value = ref[0, :, at].astype(F32)
        for p in range(1, ref.shape[0]):
            value = value + ref[p, :, at].astype(F32)
        return value

    stat = total_of(recv1, pl.ds(stat_at, HEAD))
    row_scale = lax.rsqrt((stat[:, 0:1] + stat[:, 64:65]) / width + EPSILON)

    @pl.loop(0, HEADS)
    def _(h):
        at = pl.ds(pl.multiple_of(h * HEAD, HEAD), HEAD)
        s["q"][h] = rope(total_of(recv1, at) * row_scale, own_table).astype(BF16)

    new_key = rope(total_of(recv1, pl.ds(qw, HEAD)) * row_scale, own_table).astype(BF16)
    new_value = (total_of(recv1, pl.ds(qw + HEAD, HEAD)) * row_scale).astype(BF16)
    queries = s["q"][...].reshape(HEADS * 16, HEAD)
    keys = jnp.concatenate([new_key.astype(F32)] * HEADS, axis=0)
    values = jnp.concatenate([new_value.astype(F32)] * HEADS, axis=0)
    own = jnp.sum(queries.astype(F32) * keys, axis=1, keepdims=True) * scale

    total = total_of(recv1, pl.ds(ext_at, HEAD))
    tail = total_of(recv1, pl.ds(ext_at + HEAD, HEAD))
    far_scale = lax.rsqrt((tail[:, 0:1] + tail[:, 32:33]) / width + EPSILON)
    low8 = lax.broadcasted_iota(jnp.int32, (16, HEAD), 0) < 8
    places = jnp.where(
        low8, recv1[0, :, ext_at + HEAD :].astype(F32), recv1[mid, :, ext_at + HEAD :].astype(F32)
    )
    far_table = rope_tables(places[:, 64:65] * 256.0 + places[:, 96:97], inv_ref[...])
    far_query = rope(total * far_scale, far_table).astype(BF16)

    chunk = min(512, slots)
    n_chunk = slots // chunk
    contract = (((1,), (1,)), ((), ()))
    low_chunk = lax.broadcasted_iota(jnp.int32, (16, chunk), 0) < 8
    live = jnp.where(low_chunk, split_ref[0, 0], split_ref[0, 1])

    def scores_of(c, best):
        far_best, near_best = best
        at = pl.ds(pl.multiple_of(c * chunk, chunk), chunk)
        a = lax.dot_general(far_query, far[0, at, 0:HEAD], contract, preferred_element_type=F32)
        b = lax.dot_general(far_query, far[1, at, 0:HEAD], contract, preferred_element_type=F32)
        slot = lax.broadcasted_iota(jnp.int32, (16, chunk), 1) + c * chunk
        value = jnp.where(slot < live, jnp.where(low_chunk, a, b) * scale, NEG)
        s["fscore"][:, at] = value
        far_best = jnp.maximum(far_best, jnp.max(value, axis=1, keepdims=True))
        near = lax.dot_general(queries, pack[at, 0:HEAD], contract, preferred_element_type=F32)
        slot = lax.broadcasted_iota(jnp.int32, (HEADS * 16, chunk), 1) + c * chunk
        value = jnp.where((slot >= seg_start) & (slot < seg_end), near * scale, NEG)
        s["score"][:, at] = value
        return far_best, jnp.maximum(near_best, jnp.max(value, axis=1, keepdims=True))

    far_max, row_max = lax.fori_loop(0, n_chunk, scores_of, (jnp.full((16, 1), NEG, F32), own))
    own_weight = jnp.exp(own - row_max).astype(BF16).astype(F32)

    def sums_of(c, carry):
        far_totals, far_sum, totals, summed = carry
        at = pl.ds(pl.multiple_of(c * chunk, chunk), chunk)
        w = jnp.exp(s["fscore"][:, at] - far_max).astype(BF16)
        a = jnp.dot(w, far[0, at, HEAD:], preferred_element_type=F32)
        b = jnp.dot(w, far[1, at, HEAD:], preferred_element_type=F32)
        far_totals = far_totals + jnp.sum(w.astype(F32), axis=1, keepdims=True)
        far_sum = far_sum + jnp.where(low8, a, b)
        w = jnp.exp(s["score"][:, at] - row_max).astype(BF16)
        summed = summed + jnp.dot(w, pack[at, HEAD:], preferred_element_type=F32)
        return far_totals, far_sum, totals + jnp.sum(w.astype(F32), axis=1, keepdims=True), summed

    far_totals, far_sum, totals, summed = lax.fori_loop(
        0, n_chunk, sums_of,
        (jnp.zeros((16, 1), F32), jnp.zeros((16, HEAD), F32), own_weight, own_weight * values),
    )
    far_out = far_sum / far_totals
    far_lse = jnp.broadcast_to(far_max + jnp.log(far_totals), (16, HEAD))
    attended = summed / totals
    s["att"][...] = attended
    s["lse"][...] = jnp.broadcast_to(row_max + jnp.log(totals), (HEADS * 16, HEAD))
    mixed = s["mixed"]
    for h in range(HEADS):
        mixed[me, :, h * HEAD : (h + 1) * HEAD] = attended[h * 16 : (h + 1) * 16].astype(BF16)

    first_out = s["att"][pl.ds(0, HEADS, stride=16), :]
    first_lse = s["lse"][pl.ds(0, HEADS, stride=16), :]
    near_out = jnp.concatenate([first_out, first_out], axis=0)
    near_lse = jnp.concatenate([first_lse, first_lse], axis=0)
    owned = jnp.where(low8, 0, mid) == me
    peak = jnp.maximum(far_lse, near_lse)
    fa = jnp.exp(far_lse - peak)
    na = jnp.exp(near_lse - peak)
    part_out = jnp.where(owned, (fa * far_out + na * near_out) / (fa + na), far_out)
    part_lse = jnp.where(owned, peak + jnp.log(fa + na), far_lse)
    high = part_lse.astype(BF16).astype(F32)
    middle = (part_lse - high).astype(BF16).astype(F32)
    low = part_lse - high - middle
    mixed[me, :, qw : qw + HEAD] = part_out.astype(BF16)
    mixed[me, :, qw + HEAD :] = jnp.where(lane16 < 32, high, jnp.where(lane16 < 64, middle, low)).astype(BF16)
    spread_req("p2", lambda p: mixed.at[me], mixed)
    sent("p1", s["send1"], n_req - 1)
    load_wo.wait()
    arrived("p2", mixed, n_req - 1)

    parts = []
    for p in range(n_req):
        part = mixed[p, :, qw + HEAD :].astype(F32)
        parts.append(part[:, 0:1] + part[:, 32:33] + part[:, 64:65])
    peak = functools.reduce(jnp.maximum, parts)
    den = jnp.zeros((16, 1), F32)
    num = jnp.zeros((16, HEAD), F32)
    for p in range(n_req):
        w = jnp.exp(parts[p] - peak)
        den = den + w
        num = num + w * mixed[p, :, qw : qw + HEAD].astype(F32)
    long_out = num / den
    lhs = s["lhs"]
    lhs[...] = mixed[:, :, 0:qw]
    first = lax.broadcasted_iota(jnp.int32, (16, qw), 0) == 0
    for j in range(2):
        flat = jnp.concatenate([long_out[j * 8 + h : j * 8 + h + 1] for h in range(HEADS)], axis=1)
        block = mixed[j * mid, :, 0:qw].astype(F32)
        lhs[j * mid] = jnp.where(first, jnp.broadcast_to(flat, (16, qw)), block).astype(BF16)

    send3, recv3, res = s["send3"], s["recv3"], s["res"]
    for h in range(n_half):
        part = jnp.dot(lhs[...].reshape(rows, qw), s["wo"][:, pl.ds(h * hcols, hcols)], preferred_element_type=F32)
        send3[h] = part.astype(BF16).reshape(n_head, blk, hcols)
        spread_head("p3", lambda p, h=h: send3.at[h, p], recv3.at[h], h)
    sent("p2", mixed, n_req - 1)

    def block_total(buffer, mine, h):
        value = mine[h, mz].astype(F32)
        for k in range(1, n_head):
            value = value + buffer[h, lax.rem(mz + k, n_head)].astype(F32)
        return value

    for h in range(n_half):
        arrived("p3", recv3.at[h], n_head - 1, h)
        res[h, mz] = (xin[h, mz].astype(F32) + block_total(recv3, send3, h)).astype(BF16)
        spread_head("p4", lambda p, h=h: res.at[h, mz], res.at[h], h)
    for h in range(n_half):
        sent("p3", send3.at[h], n_head - 1, h)
    for h in range(n_half):
        arrived("p4", res.at[h], n_head - 1, h)

    squares = normed(res, gain2_ref)
    n_part = len(ff_parts)

    def along(side, k):
        if side == 0:
            c = lax.rem(mx + k, SIDE)
            return c, {"req": c * SIDE + my}
        c = lax.rem(my + k, SIDE)
        return c, {"req": mx * SIDE + c}

    coordinate = (mx, my)
    for g, (begin, end) in enumerate(ff_parts):
        buf = s[f"fs{g}"]

        @pl.loop(begin, end)
        def _(c, g=g, buf=buf, begin=begin):
            part = jnp.dot(
                s["xg"][...], s["wgu"][:, pl.ds(pl.multiple_of(c * 256, 256), 256)], preferred_element_type=F32
            ).astype(BF16).reshape(SIDE, SIDE, 16, 256)
            at = pl.ds(pl.multiple_of((c - begin) * 256, 256), 256)
            for a in range(SIDE):
                if g % 2 == 0:
                    buf[a, :, :, at] = part[a]
                else:
                    buf[a, :, :, at] = part[:, a]

        if g == 0:
            at = pl.ds((end - begin) * 256, HEAD)
            buf[:, :, :, at] = split_two(squares, lanes).reshape(SIDE, SIDE, 16, HEAD)
        for k in range(1, SIDE):
            c, peer = along(g % 2, k)
            remote(buf.at[c], s[f"fr{g}"].at[coordinate[g % 2]], "f1", g, peer).start()
    for h in range(n_half):
        sent("p4", res.at[h], n_head - 1, h)

    for g, (begin, end) in enumerate(ff_parts):
        side = g % 2
        buf, got, turn = s[f"fs{g}"], s[f"fr{g}"], s[f"ft{g}"]
        arrived("f1", got, SIDE - 1, g)
        mine = coordinate[side]

        @pl.loop(0, SIDE)
        def _(b, g=g, buf=buf, got=got, turn=turn, mine=mine, begin=begin, end=end):
            value = buf[mine, b].astype(F32)
            for k in range(1, SIDE):
                value = value + got[lax.rem(mine + k, SIDE), b].astype(F32)
            turn[b] = value.astype(BF16)
            if g == 0:
                stat = value[:, (end - begin) * 256 :]
                turn[b, :, pl.ds((end - begin) * 256, HEAD)] = split_two(stat[:, 0:1] + stat[:, 64:65], lane16)

        for k in range(1, SIDE):
            c, peer = along(1 - side, k)
            remote(turn.at[c], s[f"fu{g}"].at[coordinate[1 - side]], "f2", g, peer).start()

    ff_scale = None
    hid = (s["hid0"], s["hid1"])
    for g, (begin, end) in enumerate(ff_parts):
        side = g % 2
        turn, got = s[f"ft{g}"], s[f"fu{g}"]
        arrived("f2", got, SIDE - 1, g)
        mine = coordinate[1 - side]

        def turned(at, turn=turn, got=got, mine=mine):
            value = turn[mine, :, at].astype(F32)
            for k in range(1, SIDE):
                value = value + got[lax.rem(mine + k, SIDE), :, at].astype(F32)
            return value

        if g == 0:
            stat = turned(pl.ds((end - begin) * 256, HEAD))
            ff_scale = lax.rsqrt((stat[:, 0:1] + stat[:, 64:65]) / width + EPSILON)
        which = g // 2
        base = ff_parts[2 * which][0]
        for c in range(begin, end):
            both = turned(pl.ds((c - begin) * 256, 256)) * ff_scale
            gate, up = both[:, :HEAD], both[:, HEAD:]
            hid[which][me, :, pl.ds((c - base) * HEAD, HEAD)] = (gate / (1.0 + jnp.exp(-gate)) * up).astype(BF16)
        if g % 2 == 1:
            spread_req("p6", lambda p, which=which: hid[which].at[me], hid[which], which)
    for g in range(n_part):
        sent("f1", s[f"fs{g}"], SIDE - 1, g)
        sent("f2", s[f"ft{g}"], SIDE - 1, g)

    load_wd.wait()
    send7, recv7, oblk, out, down = s["send7"], s["recv7"], s["oblk"], s["out"], s["down"]
    wide0 = hid[0].shape[2]
    arrived("p6", hid[0], n_req - 1, 0)
    for h in range(n_half):
        at = pl.ds(h * hcols, hcols)
        down[:, at] = jnp.dot(hid[0][...].reshape(rows, wide0), s["wd"][pl.ds(0, wide0), at], preferred_element_type=F32)
    arrived("p6", hid[1], n_req - 1, 1)
    for h in range(n_half):
        at = pl.ds(h * hcols, hcols)
        part = down[:, at] + jnp.dot(
            hid[1][...].reshape(rows, ff - wide0), s["wd"][pl.ds(wide0, ff - wide0), at], preferred_element_type=F32
        )
        send7[h] = part.astype(BF16).reshape(n_head, blk, hcols)
        spread_head("p7", lambda p, h=h: send7.at[h, p], recv7.at[h], h)
    for which in range(2):
        sent("p6", hid[which], n_req - 1, which)

    def hand_over(k, h):
        return remote(oblk.at[h], xin.at[h, mz], "in", h, {"section": 1, **head_peer(k)})

    for h in range(n_half):
        arrived("p7", recv7.at[h], n_head - 1, h)
        oblk[h] = (res[h, mz].astype(F32) + block_total(recv7, send7, h)).astype(BF16)

        @pl.when(sec == 0)
        def _(h=h):
            @pl.loop(0, n_head)
            def _(k):
                hand_over(k, h).start()

        @pl.when(sec == 1)
        def _(h=h):
            out[h, mz] = oblk[h]
            spread_head("p8", lambda p: oblk.at[h], out.at[h], h)

    for h in range(n_half):
        sent("p7", send7.at[h], n_head - 1, h)

    @pl.when(sec == 0)
    def _():
        remote(xin, out, "back", 0, {"section": 1}).wait_recv()
        for h in range(n_half):
            remote(xin.at[h], xin.at[h], "in", h, {"section": 1}).wait_send()

    @pl.when(sec == 1)
    def _():
        for h in range(n_half):
            arrived("p8", out.at[h], n_head - 1, h)

    for h in range(n_half):
        out_ref[:, :, pl.ds(h * hcols, hcols)] = out[h]

    @pl.when(sec == 1)
    def _():
        for h in range(n_half):
            sent("p8", out.at[h], n_head - 1, h)
        remote(xin, out, "back", 0, {"section": 0}).wait_send()


def local(
    tokens,
    attention_gain,
    query_key_value_weight,
    head_output_weight,
    feedforward_gain,
    gate_up,
    down_weight,
    packed_cache,
    long_cache,
    lengths,
    long_split,
):
    n_req = lax.axis_size("req")
    n_head = lax.axis_size("head")
    rows, cols = tokens.shape
    blk = rows // n_head
    qkv = query_key_value_weight.shape[3]
    qw = head_output_weight.shape[2]
    ff = down_weight.shape[1]
    slots = packed_cache.shape[1]
    assert slots == long_cache.shape[2] and rows == n_req * 16 and n_req == SIDE * SIDE
    half = (2, n_head, blk, cols // 2)
    n = ff // HEAD
    cuts = (0, (2 * n + 6) // 7, (4 * n + 6) // 7, (11 * n + 12) // 14, n)
    ff_parts = tuple(zip(cuts[:-1], cuts[1:]))
    freq_ids = np.arange(HEAD // 2, dtype=np.float32)
    inverse = np.float32(1.0) / np.power(np.float32(10000.0), freq_ids * np.float32(2.0) / np.float32(HEAD))
    inverse = jnp.asarray(np.concatenate([inverse, inverse])[None].astype(np.float32))
    vmem = pl.BlockSpec(memory_space=pltpu.VMEM)
    hbm = pl.BlockSpec(memory_space=pl.ANY)
    smem = pl.BlockSpec(memory_space=pltpu.SMEM)
    scratch = dict(
        wqkv=pltpu.VMEM((cols, qkv), BF16),
        wo=pltpu.VMEM((qw, cols), BF16),
        raw=pltpu.VMEM((cols, 2, ff), BF16),
        wgu=pltpu.VMEM((cols, 2 * ff), BF16),
        wd=pltpu.VMEM((ff, cols), BF16),
        pack=pltpu.VMEM((slots, 2 * HEAD), BF16),
        far=pltpu.VMEM((2, slots, 2 * HEAD), BF16),
        xin=pltpu.VMEM(half, BF16),
        xg=pltpu.VMEM((rows, cols), BF16),
        send1=pltpu.VMEM((n_req, 16, qkv + 3 * HEAD), BF16),
        recv1=pltpu.VMEM((n_req, 16, qkv + 3 * HEAD), BF16),
        ext=pltpu.VMEM((16, 2 * HEAD), F32),
        q=pltpu.VMEM((HEADS, 16, HEAD), BF16),
        score=pltpu.VMEM((HEADS * 16, slots), F32),
        fscore=pltpu.VMEM((16, slots), F32),
        att=pltpu.VMEM((HEADS * 16, HEAD), F32),
        lse=pltpu.VMEM((HEADS * 16, HEAD), F32),
        mixed=pltpu.VMEM((n_req, 16, qw + 2 * HEAD), BF16),
        lhs=pltpu.VMEM((n_req, 16, qw), BF16),
        send3=pltpu.VMEM(half, BF16),
        recv3=pltpu.VMEM(half, BF16),
        res=pltpu.VMEM(half, BF16),
        hid0=pltpu.VMEM((n_req, 16, cuts[2] * HEAD), BF16),
        hid1=pltpu.VMEM((n_req, 16, (n - cuts[2]) * HEAD), BF16),
        down=pltpu.VMEM((rows, cols), F32),
        send7=pltpu.VMEM(half, BF16),
        recv7=pltpu.VMEM(half, BF16),
        oblk=pltpu.VMEM((2, blk, cols // 2), BF16),
        out=pltpu.VMEM(half, BF16),
        wsem=pltpu.SemaphoreType.DMA((8,)),
    )
    for g, (begin, end) in enumerate(ff_parts):
        wide = (end - begin) * 256 + (HEAD if g == 0 else 0)
        scratch[f"fs{g}"] = pltpu.VMEM((SIDE, SIDE, 16, wide), BF16)
        scratch[f"fr{g}"] = pltpu.VMEM((SIDE, SIDE, 16, wide), BF16)
        scratch[f"ft{g}"] = pltpu.VMEM((SIDE, 16, wide), BF16)
        scratch[f"fu{g}"] = pltpu.VMEM((SIDE, 16, wide), BF16)
    for name, count in dict(p1=1, p2=1, p3=2, p4=2, f1=4, f2=4, p6=2, p7=2, p8=2, **{"in": 2}, back=1).items():
        scratch["ss_" + name] = pltpu.SemaphoreType.DMA((count,))
        scratch["rs_" + name] = pltpu.SemaphoreType.DMA((count,))
    names = list(scratch)

    def body(*refs):
        plain, rest = refs[:13], refs[13:]
        kernel((n_req, n_head, cols * n_req), ff_parts, *plain, dict(zip(names, rest)))

    out = pl.pallas_call(
        body,
        out_shape=jax.ShapeDtypeStruct((n_head, blk, cols), BF16),
        in_specs=[smem, hbm, vmem, hbm, hbm, vmem, hbm, hbm, hbm, hbm, vmem, vmem],
        out_specs=vmem,
        scratch_shapes=[scratch[name] for name in names],
        compiler_params=pltpu.CompilerParams(
            collective_id=0, has_side_effects=True, vmem_limit_bytes=56 * 2**20
        ),
        name="two_layers",
    )(
        long_split.T,
        tokens.reshape(n_head, blk, cols),
        attention_gain,
        query_key_value_weight.reshape(cols, qkv),
        head_output_weight.reshape(qw, cols),
        feedforward_gain,
        gate_up.reshape(cols, 2, ff),
        down_weight.reshape(ff, cols),
        packed_cache.reshape(slots, 2 * HEAD),
        long_cache.reshape(2, slots, 2 * HEAD),
        lengths,
        inverse,
    )
    return out.reshape(1, rows, cols)


def solution(mesh):
    placed = (
        P(None, "req"),
        P("section", "req"),
        P("section", "req", "head", None),
        P("section", "head", None, "req"),
        P("section", "req"),
        P("section", "req", None, "head"),
        P("section", "head", "req"),
        P("section", "req", "head", None),
        P("section", None, "req", "head", None),
        P("req", None),
        P(None, "req"),
    )
    return jax.shard_map(
        local, mesh=mesh, in_specs=placed, out_specs=P("section", None, "req"), check_vma=False
    )
```

time: 1030 us -> 148 us (0.14)
  waiting for transfers between devices: 677 us -> 0 us
  blocking collectives: 278 us -> 0 us
  Pallas kernels: 0 us -> 146 us
  matrix products: 31.7 us -> 0 us
  other arithmetic: 17.4 us -> 0 us
  between operations: 13.9 us -> 0.01 us
    psum x4 -> x0, waiting for transfers between devices: 338 us -> none  [head_total(): return lax.psum(values, 'head')]
    reduce_scatter x4 -> x0, waiting for transfers between devices: 333 us -> none  [rows_project(): lax.psum_scatter(term_fn(jnp.int32(0), row_count * lax.axis_size('req')),...]
    all_gather x16 -> x0, blocking collectives: 278 us -> none  [the longest x10 171 us: merged(): gathered = jax.tree.map(lambda a: lax.all_gather(a, axis), part)]
    pallas_call x0 -> x1, Pallas kernels: none -> 146 us  [local(): pl.pallas_call(body, out_shape=jax.ShapeDtypeStruct((n_head, blk, cols),...]
    dot_general x18 -> x0, matrix products: 31.7 us -> none  [the longest x2 10.1 us: ff_term(): return jnp.dot(normed_two, ff_weights, preferred_element_type=jnp.float32)]
  transfers between devices with their start and end apart: 9 -> 0, of which waited for: 9 -> 0; matrix products, arithmetic and copies ran while one was open for 1% -> 0% of each run, Pallas kernels for 0% -> 0%
where the time goes in v2:
time: 148 us; the launch traced here: 147 us
  Pallas kernels  146 us (99%)
  local copies, waits for them, and re-layouts  1.67 us (1%)
    pallas_call x1, Pallas kernels, local(): pl.pallas_call(body, out_shape=jax.ShapeDtypeStruct((n_head, blk, cols),...  146 us

profile of v2, /device:TPU:1, one launch (start us, length us, event | category | flops | bytes accessed | tf_op | source)
XLA Modules:
  0.0 147.4 jit_solution(2567727819221391834)
XLA Ops:
  0.0 145.7 %two_layers.1 = bf16[8,32,512]{2,1,0:T(8,128)(2,1)} custom-call(s32[1,2]{1,0:T(1,128)} %bitcast.17, bf16[8,32,512]{2,1,0:T(8,128)(2,1)} %bitcast.16, bf16[1,512]{1,0:T(2,128)(2,1)} %refs_2_.1, bf16[512,1280]{1,0:T(8,128)(2,1)} %bitcast.12, bf16[1024,512]{1,0:T(8,128)(2,1)} %bitcast.14, bf16[1,512]{1,0:T(2,128)(2,1)} %refs_5_.1, ...), custom_call_target="tpu_custom_call" | custom-call | tf_op jit(solution)/shard_map/two_layers/pallas_call | solution.py:586
  145.7 1.7 %copy.14 = bf16[1,256,512]{2,1,0:T(8,128)(2,1)} copy(bf16[1,256,512]{2,1,0:T(8,128)(2,1)} %bitcast.13) | data formatting | bytes 524288

commit v3 on v2

--- a/solution.py
+++ b/solution.py
@@ -18,6 +18,10 @@
 BF16 = jnp.bfloat16
 MESH = pl.DeviceIdType.MESH
 SIDE = 4
+FAR_FIRST = sorted(
+    ((a, b) for a in range(SIDE) for b in range(SIDE) if a or b),
+    key=lambda d: (-(d[0] > 0) - (d[1] > 0), -min(d[0], SIDE - d[0]) - min(d[1], SIDE - d[1]), d),
+)
 
 
 def split_two(value, lanes):
@@ -54,8 +58,8 @@
     ff = s["wd"].shape[0]
     scale = 1.0 / math.sqrt(HEAD)
     mid = n_req // 2
-    stat_at = qw + 2 * HEAD
-    ext_at = stat_at + HEAD
+    ext_at = qw + 2 * HEAD
+    stat_at = ext_at + HEAD
 
     def remote(source, target, name, where, peer):
         return pltpu.make_async_remote_copy(
@@ -63,21 +67,21 @@
             device_id=peer, device_id_type=MESH,
         )
 
-    def req_peer(k):
-        return {"req": lax.rem(mx + lax.div(k, SIDE), SIDE) * SIDE + lax.rem(my + lax.rem(k, SIDE), SIDE)}
+    def req_peer(step):
+        return {"req": lax.rem(mx + step[0], SIDE) * SIDE + lax.rem(my + step[1], SIDE)}
+
+    ring = sorted(range(1, n_head), key=lambda k: (-min(k, n_head - k), k))
 
     def head_peer(k):
         return {"head": lax.rem(mz + k, n_head)}
 
     def spread_req(name, source, target, where=0):
-        @pl.loop(1, n_req)
-        def _(k):
-            peer = req_peer(k)
+        for step in FAR_FIRST:
+            peer = req_peer(step)
             remote(source(peer["req"]), target.at[me], name, where, peer).start()
 
     def spread_head(name, source, target, where=0):
-        @pl.loop(1, n_head)
-        def _(k):
+        for k in ring:
             peer = head_peer(k)
             remote(source(peer["head"]), target.at[mz], name, where, peer).start()
 
@@ -107,16 +111,11 @@
 
     barrier = pltpu.get_barrier_semaphore()
 
-    @pl.loop(1, n_req)
-    def _(k):
-        pl.semaphore_signal(barrier, inc=1, device_id=req_peer(k), device_id_type=MESH)
-
-    @pl.loop(1, n_head)
-    def _(k):
+    for step in FAR_FIRST:
+        pl.semaphore_signal(barrier, inc=1, device_id=req_peer(step), device_id_type=MESH)
+    for k in ring:
         pl.semaphore_signal(barrier, inc=1, device_id=head_peer(k), device_id_type=MESH)
-
-    @pl.loop(0, n_head)
-    def _(k):
+    for k in ring + [0]:
         pl.semaphore_signal(barrier, inc=1, device_id={"section": 1 - sec, **head_peer(k)}, device_id_type=MESH)
 
     for other in (load_raw, load_pack, load_far, load_wo, load_wd):
@@ -145,10 +144,9 @@
 
     def first_products():
         squares = normed(xin, gain1_ref)
-        s["send1"][:, :, stat_at : stat_at + HEAD] = split_two(squares, lanes).reshape(n_req, 16, HEAD)
         load_qkv.wait()
 
-        @pl.loop(0, stat_at // 256)
+        @pl.loop(0, ext_at // 256)
         def _(c):
             at = pl.ds(pl.multiple_of(c * 256, 256), 256)
             part = jnp.dot(s["xg"][...], s["wqkv"][:, at], preferred_element_type=F32)
@@ -156,21 +154,24 @@
 
         ext = s["ext"]
         for j in range(2):
-            row = s["send1"][j * mid].astype(F32)[0:1]
+            row = s["send1"][j * mid, :, 0:qw].astype(F32)[0:1]
             for h in range(HEADS):
-                ext[j * 8 + h : j * 8 + h + 1, 0:HEAD] = row[:, h * HEAD : (h + 1) * HEAD]
-            ext[j * 8 : j * 8 + 8, HEAD:] = jnp.broadcast_to(row[:, stat_at : stat_at + HEAD], (8, HEAD))
+                ext[j * 8 + h : j * 8 + h + 1, :] = row[:, h * HEAD : (h + 1) * HEAD]
+        head = ext[...].astype(BF16)
         first = position[0:1]
         upper = jnp.floor(first * (1.0 / 256.0))
         lower = first - 256.0 * upper
-        tail = ext[:, HEAD:]
-        stats = jnp.where(lane16 < 32, tail[:, 0:1], tail[:, 64:65])
-        places = jnp.where(lane16 < 96, upper, lower)
-        tail = jnp.where(lane16 < 64, stats, places).astype(BF16)
-        head = ext[:, 0:HEAD].astype(BF16)
+        row16 = lax.broadcasted_iota(jnp.int32, (16, HEAD), 0)
+        far_squares = jnp.where(row16 < 8, squares[0:1], squares[mid * 16 : mid * 16 + 1])
+        far_high = far_squares.astype(BF16).astype(F32)
+        common = jnp.where(
+            lane16 < 80, far_high, jnp.where(lane16 < 96, far_squares - far_high, jnp.where(lane16 < 112, upper, lower))
+        )
+        high = squares.astype(BF16).astype(F32)
+        pair = jnp.where(lanes < 32, high, squares - high).reshape(n_req, 16, HEAD)
         for g in range(n_req):
             s["send1"][g, :, ext_at : ext_at + HEAD] = head
-            s["send1"][g, :, ext_at + HEAD :] = tail
+            s["send1"][g, :, stat_at : stat_at + HEAD] = jnp.where(lane16 < 64, pair[g], common).astype(BF16)
 
     def split_gate():
         load_raw.wait()
@@ -225,7 +226,7 @@
         return value
 
     stat = total_of(recv1, pl.ds(stat_at, HEAD))
-    row_scale = lax.rsqrt((stat[:, 0:1] + stat[:, 64:65]) / width + EPSILON)
+    row_scale = lax.rsqrt((stat[:, 0:1] + stat[:, 32:33]) / width + EPSILON)
 
     @pl.loop(0, HEADS)
     def _(h):
@@ -240,13 +241,12 @@
     own = jnp.sum(queries.astype(F32) * keys, axis=1, keepdims=True) * scale
 
     total = total_of(recv1, pl.ds(ext_at, HEAD))
-    tail = total_of(recv1, pl.ds(ext_at + HEAD, HEAD))
-    far_scale = lax.rsqrt((tail[:, 0:1] + tail[:, 32:33]) / width + EPSILON)
+    far_scale = lax.rsqrt((stat[:, 64:65] + stat[:, 80:81]) / width + EPSILON)
     low8 = lax.broadcasted_iota(jnp.int32, (16, HEAD), 0) < 8
     places = jnp.where(
-        low8, recv1[0, :, ext_at + HEAD :].astype(F32), recv1[mid, :, ext_at + HEAD :].astype(F32)
+        low8, recv1[0, :, stat_at : stat_at + HEAD].astype(F32), recv1[mid, :, stat_at : stat_at + HEAD].astype(F32)
     )
-    far_table = rope_tables(places[:, 64:65] * 256.0 + places[:, 96:97], inv_ref[...])
+    far_table = rope_tables(places[:, 96:97] * 256.0 + places[:, 112:113], inv_ref[...])
     far_query = rope(total * far_scale, far_table).astype(BF16)
 
     chunk = min(512, slots)
@@ -471,8 +471,7 @@
 
         @pl.when(sec == 0)
         def _(h=h):
-            @pl.loop(0, n_head)
-            def _(k):
+            for k in ring + [0]:
                 hand_over(k, h).start()
 
         @pl.when(sec == 1)
@@ -528,7 +527,7 @@
     assert slots == long_cache.shape[2] and rows == n_req * 16 and n_req == SIDE * SIDE
     half = (2, n_head, blk, cols // 2)
     n = ff // HEAD
-    cuts = (0, (2 * n + 6) // 7, (4 * n + 6) // 7, (11 * n + 12) // 14, n)
+    cuts = (0, 3 * n // 14, 6 * n // 14, 10 * n // 14, n)
     ff_parts = tuple(zip(cuts[:-1], cuts[1:]))
     freq_ids = np.arange(HEAD // 2, dtype=np.float32)
     inverse = np.float32(1.0) / np.power(np.float32(10000.0), freq_ids * np.float32(2.0) / np.float32(HEAD))
@@ -546,9 +545,9 @@
         far=pltpu.VMEM((2, slots, 2 * HEAD), BF16),
         xin=pltpu.VMEM(half, BF16),
         xg=pltpu.VMEM((rows, cols), BF16),
-        send1=pltpu.VMEM((n_req, 16, qkv + 3 * HEAD), BF16),
-        recv1=pltpu.VMEM((n_req, 16, qkv + 3 * HEAD), BF16),
-        ext=pltpu.VMEM((16, 2 * HEAD), F32),
+        send1=pltpu.VMEM((n_req, 16, qkv + 2 * HEAD), BF16),
+        recv1=pltpu.VMEM((n_req, 16, qkv + 2 * HEAD), BF16),
+        ext=pltpu.VMEM((16, HEAD), F32),
         q=pltpu.VMEM((HEADS, 16, HEAD), BF16),
         score=pltpu.VMEM((HEADS * 16, slots), F32),
         fscore=pltpu.VMEM((16, slots), F32),

time: 148 us -> 133 us (0.90)
  Pallas kernels: 146 us -> 131 us
    pallas_call x1, Pallas kernels: 146 us -> 131 us  [local(): pl.pallas_call(body, out_shape=jax.ShapeDtypeStruct((n_head, blk, cols),...]
where the time goes in v3:
time: 133 us
  Pallas kernels  131 us (98%)
  local copies, waits for them, and re-layouts  1.67 us (1%)
    pallas_call x1, Pallas kernels, local(): pl.pallas_call(body, out_shape=jax.ShapeDtypeStruct((n_head, blk, cols),...  131 us

profile of v3, /device:TPU:1, one launch (start us, length us, event | category | flops | bytes accessed | tf_op | source)
XLA Modules:
  0.0 133.1 jit_solution(12739551279091264444)
XLA Ops:
  0.0 131.4 %two_layers.1 = bf16[8,32,512]{2,1,0:T(8,128)(2,1)} custom-call(s32[1,2]{1,0:T(1,128)} %bitcast.17, bf16[8,32,512]{2,1,0:T(8,128)(2,1)} %bitcast.16, bf16[1,512]{1,0:T(2,128)(2,1)} %refs_2_.1, bf16[512,1280]{1,0:T(8,128)(2,1)} %bitcast.12, bf16[1024,512]{1,0:T(8,128)(2,1)} %bitcast.14, bf16[1,512]{1,0:T(2,128)(2,1)} %refs_5_.1, ...), custom_call_target="tpu_custom_call" | custom-call | tf_op jit(solution)/shard_map/two_layers/pallas_call | solution.py:585
  131.4 1.7 %copy.14 = bf16[1,256,512]{2,1,0:T(8,128)(2,1)} copy(bf16[1,256,512]{2,1,0:T(8,128)(2,1)} %bitcast.13) | data formatting | bytes 524288

commit v4 on v3

--- a/solution.py
+++ b/solution.py
@@ -24,6 +24,11 @@
 )
 
 
+PIECES = 2
+PARTS = (1, 1, 2, 2, 2, 2, 2, 2)
+SETS = ((0, 1, 2, 3), (4, 5), (6, 7))
+
+
 def split_two(value, lanes):
     high = value.astype(BF16).astype(F32)
     return jnp.where(lanes < 64, high, value - high).astype(BF16)
@@ -41,7 +46,7 @@
     return jnp.cos(angles), jnp.where(lane < HEAD // 2, -sine, sine)
 
 
-def kernel(dims, ff_parts, split_ref, tok_hbm, gain1_ref, wqkv_hbm, wo_hbm, gain2_ref, raw_hbm, wd_hbm, pack_hbm, far_hbm,
+def kernel(dims, ff_parts, wides, split_ref, tok_hbm, gain1_ref, wqkv_hbm, wo_hbm, gain2_ref, raw_hbm, wd_hbm, pack_hbm, far_hbm,
            len_ref, inv_ref, out_ref, scratch):
     n_req, n_head, width = dims
     s = scratch
@@ -111,12 +116,16 @@
 
     barrier = pltpu.get_barrier_semaphore()
 
+    def greet_section():
+        for k in ring + [0]:
+            pl.semaphore_signal(barrier, inc=1, device_id={"section": 1 - sec, **head_peer(k)}, device_id_type=MESH)
+
+    pl.when(sec == 1)(greet_section)
     for step in FAR_FIRST:
         pl.semaphore_signal(barrier, inc=1, device_id=req_peer(step), device_id_type=MESH)
     for k in ring:
         pl.semaphore_signal(barrier, inc=1, device_id=head_peer(k), device_id_type=MESH)
-    for k in ring + [0]:
-        pl.semaphore_signal(barrier, inc=1, device_id={"section": 1 - sec, **head_peer(k)}, device_id_type=MESH)
+    pl.when(sec == 0)(greet_section)
 
     for other in (load_raw, load_pack, load_far, load_wo, load_wd):
         other.start()
@@ -146,7 +155,7 @@
         squares = normed(xin, gain1_ref)
         load_qkv.wait()
 
-        @pl.loop(0, ext_at // 256)
+        @pl.loop(0, ext_at // 256, unroll=True)
         def _(c):
             at = pl.ds(pl.multiple_of(c * 256, 256), 256)
             part = jnp.dot(s["xg"][...], s["wqkv"][:, at], preferred_element_type=F32)
@@ -228,9 +237,8 @@
     stat = total_of(recv1, pl.ds(stat_at, HEAD))
     row_scale = lax.rsqrt((stat[:, 0:1] + stat[:, 32:33]) / width + EPSILON)
 
-    @pl.loop(0, HEADS)
-    def _(h):
-        at = pl.ds(pl.multiple_of(h * HEAD, HEAD), HEAD)
+    for h in range(HEADS):
+        at = pl.ds(h * HEAD, HEAD)
         s["q"][h] = rope(total_of(recv1, at) * row_scale, own_table).astype(BF16)
 
     new_key = rope(total_of(recv1, pl.ds(qw, HEAD)) * row_scale, own_table).astype(BF16)
@@ -270,7 +278,7 @@
         s["score"][:, at] = value
         return far_best, jnp.maximum(near_best, jnp.max(value, axis=1, keepdims=True))
 
-    far_max, row_max = lax.fori_loop(0, n_chunk, scores_of, (jnp.full((16, 1), NEG, F32), own))
+    far_max, row_max = lax.fori_loop(0, n_chunk, scores_of, (jnp.full((16, 1), NEG, F32), own), unroll=True)
     own_weight = jnp.exp(own - row_max).astype(BF16).astype(F32)
 
     def sums_of(c, carry):
@@ -288,6 +296,7 @@
     far_totals, far_sum, totals, summed = lax.fori_loop(
         0, n_chunk, sums_of,
         (jnp.zeros((16, 1), F32), jnp.zeros((16, HEAD), F32), own_weight, own_weight * values),
+        unroll=True,
     )
     far_out = far_sum / far_totals
     far_lse = jnp.broadcast_to(far_max + jnp.log(far_totals), (16, HEAD))
@@ -374,7 +383,7 @@
     for g, (begin, end) in enumerate(ff_parts):
         buf = s[f"fs{g}"]
 
-        @pl.loop(begin, end)
+        @pl.loop(begin, end, unroll=True)
         def _(c, g=g, buf=buf, begin=begin):
             part = jnp.dot(
                 s["xg"][...], s["wgu"][:, pl.ds(pl.multiple_of(c * 256, 256), 256)], preferred_element_type=F32
@@ -389,7 +398,7 @@
         if g == 0:
             at = pl.ds((end - begin) * 256, HEAD)
             buf[:, :, :, at] = split_two(squares, lanes).reshape(SIDE, SIDE, 16, HEAD)
-        for k in range(1, SIDE):
+        for k in (2, 1, 3):
             c, peer = along(g % 2, k)
             remote(buf.at[c], s[f"fr{g}"].at[coordinate[g % 2]], "f1", g, peer).start()
     for h in range(n_half):
@@ -401,7 +410,7 @@
         arrived("f1", got, SIDE - 1, g)
         mine = coordinate[side]
 
-        @pl.loop(0, SIDE)
+        @pl.loop(0, SIDE, unroll=True)
         def _(b, g=g, buf=buf, got=got, turn=turn, mine=mine, begin=begin, end=end):
             value = buf[mine, b].astype(F32)
             for k in range(1, SIDE):
@@ -411,12 +420,12 @@
                 stat = value[:, (end - begin) * 256 :]
                 turn[b, :, pl.ds((end - begin) * 256, HEAD)] = split_two(stat[:, 0:1] + stat[:, 64:65], lane16)
 
-        for k in range(1, SIDE):
+        for k in (2, 1, 3):
             c, peer = along(1 - side, k)
             remote(turn.at[c], s[f"fu{g}"].at[coordinate[1 - side]], "f2", g, peer).start()
 
     ff_scale = None
-    hid = (s["hid0"], s["hid1"])
+    hid = [s[f"hid{w}"] for w in range(len(SETS))]
     for g, (begin, end) in enumerate(ff_parts):
         side = g % 2
         turn, got = s[f"ft{g}"], s[f"fu{g}"]
@@ -432,13 +441,13 @@
         if g == 0:
             stat = turned(pl.ds((end - begin) * 256, HEAD))
             ff_scale = lax.rsqrt((stat[:, 0:1] + stat[:, 64:65]) / width + EPSILON)
-        which = g // 2
-        base = ff_parts[2 * which][0]
+        which = next(w for w, members in enumerate(SETS) if g in members)
+        base = ff_parts[SETS[which][0]][0]
         for c in range(begin, end):
             both = turned(pl.ds((c - begin) * 256, 256)) * ff_scale
             gate, up = both[:, :HEAD], both[:, HEAD:]
             hid[which][me, :, pl.ds((c - base) * HEAD, HEAD)] = (gate / (1.0 + jnp.exp(-gate)) * up).astype(BF16)
-        if g % 2 == 1:
+        if g == SETS[which][-1]:
             spread_req("p6", lambda p, which=which: hid[which].at[me], hid[which], which)
     for g in range(n_part):
         sent("f1", s[f"fs{g}"], SIDE - 1, g)
@@ -446,20 +455,23 @@
 
     load_wd.wait()
     send7, recv7, oblk, out, down = s["send7"], s["recv7"], s["oblk"], s["out"], s["down"]
-    wide0 = hid[0].shape[2]
-    arrived("p6", hid[0], n_req - 1, 0)
-    for h in range(n_half):
-        at = pl.ds(h * hcols, hcols)
-        down[:, at] = jnp.dot(hid[0][...].reshape(rows, wide0), s["wd"][pl.ds(0, wide0), at], preferred_element_type=F32)
-    arrived("p6", hid[1], n_req - 1, 1)
-    for h in range(n_half):
-        at = pl.ds(h * hcols, hcols)
-        part = down[:, at] + jnp.dot(
-            hid[1][...].reshape(rows, ff - wide0), s["wd"][pl.ds(wide0, ff - wide0), at], preferred_element_type=F32
-        )
-        send7[h] = part.astype(BF16).reshape(n_head, blk, hcols)
-        spread_head("p7", lambda p, h=h: send7.at[h, p], recv7.at[h], h)
-    for which in range(2):
+    done = 0
+    for which, wide in enumerate(wides):
+        arrived("p6", hid[which], n_req - 1, which)
+        for h in range(n_half):
+            at = pl.ds(h * hcols, hcols)
+            part = jnp.dot(
+                hid[which][...].reshape(rows, wide), s["wd"][pl.ds(done, wide), at], preferred_element_type=F32
+            )
+            if which > 0:
+                part = down[:, at] + part
+            if which < len(SETS) - 1:
+                down[:, at] = part
+            else:
+                send7[h] = part.astype(BF16).reshape(n_head, blk, hcols)
+                spread_head("p7", lambda p, h=h: send7.at[h, p], recv7.at[h], h)
+        done += wide
+    for which in range(len(SETS)):
         sent("p6", hid[which], n_req - 1, which)
 
     def hand_over(k, h):
@@ -525,10 +537,11 @@
     ff = down_weight.shape[1]
     slots = packed_cache.shape[1]
     assert slots == long_cache.shape[2] and rows == n_req * 16 and n_req == SIDE * SIDE
-    half = (2, n_head, blk, cols // 2)
+    half = (PIECES, n_head, blk, cols // PIECES)
     n = ff // HEAD
-    cuts = (0, 3 * n // 14, 6 * n // 14, 10 * n // 14, n)
+    cuts = [sum(PARTS[:g]) * n // sum(PARTS) for g in range(len(PARTS) + 1)]
     ff_parts = tuple(zip(cuts[:-1], cuts[1:]))
+    wides = [(ff_parts[members[-1]][1] - ff_parts[members[0]][0]) * HEAD for members in SETS]
     freq_ids = np.arange(HEAD // 2, dtype=np.float32)
     inverse = np.float32(1.0) / np.power(np.float32(10000.0), freq_ids * np.float32(2.0) / np.float32(HEAD))
     inverse = jnp.asarray(np.concatenate([inverse, inverse])[None].astype(np.float32))
@@ -558,29 +571,32 @@
         send3=pltpu.VMEM(half, BF16),
         recv3=pltpu.VMEM(half, BF16),
         res=pltpu.VMEM(half, BF16),
-        hid0=pltpu.VMEM((n_req, 16, cuts[2] * HEAD), BF16),
-        hid1=pltpu.VMEM((n_req, 16, (n - cuts[2]) * HEAD), BF16),
         down=pltpu.VMEM((rows, cols), F32),
         send7=pltpu.VMEM(half, BF16),
         recv7=pltpu.VMEM(half, BF16),
-        oblk=pltpu.VMEM((2, blk, cols // 2), BF16),
+        oblk=pltpu.VMEM((PIECES, blk, cols // PIECES), BF16),
         out=pltpu.VMEM(half, BF16),
-        wsem=pltpu.SemaphoreType.DMA((8,)),
+        wsem=pltpu.SemaphoreType.DMA((6 + PIECES,)),
     )
+    for w, wide in enumerate(wides):
+        scratch[f"hid{w}"] = pltpu.VMEM((n_req, 16, wide), BF16)
     for g, (begin, end) in enumerate(ff_parts):
         wide = (end - begin) * 256 + (HEAD if g == 0 else 0)
         scratch[f"fs{g}"] = pltpu.VMEM((SIDE, SIDE, 16, wide), BF16)
         scratch[f"fr{g}"] = pltpu.VMEM((SIDE, SIDE, 16, wide), BF16)
         scratch[f"ft{g}"] = pltpu.VMEM((SIDE, 16, wide), BF16)
         scratch[f"fu{g}"] = pltpu.VMEM((SIDE, 16, wide), BF16)
-    for name, count in dict(p1=1, p2=1, p3=2, p4=2, f1=4, f2=4, p6=2, p7=2, p8=2, **{"in": 2}, back=1).items():
+    for name, count in dict(
+        p1=1, p2=1, p3=PIECES, p4=PIECES, f1=len(PARTS), f2=len(PARTS), p6=len(SETS), p7=PIECES, p8=PIECES,
+        **{"in": PIECES}, back=1,
+    ).items():
         scratch["ss_" + name] = pltpu.SemaphoreType.DMA((count,))
         scratch["rs_" + name] = pltpu.SemaphoreType.DMA((count,))
     names = list(scratch)
 
     def body(*refs):
         plain, rest = refs[:13], refs[13:]
-        kernel((n_req, n_head, cols * n_req), ff_parts, *plain, dict(zip(names, rest)))
+        kernel((n_req, n_head, cols * n_req), ff_parts, wides, *plain, dict(zip(names, rest)))
 
     out = pl.pallas_call(
         body,

time: 133 us -> 124 us (0.932)
  Pallas kernels: 131 us -> 122 us
    pallas_call x1, Pallas kernels: 131 us -> 122 us  [local(): pl.pallas_call(body, out_shape=jax.ShapeDtypeStruct((n_head, blk, cols),...]
where the time goes in v4:
time: 124 us
  Pallas kernels  122 us (98%)
  local copies, waits for them, and re-layouts  1.67 us (1%)
    pallas_call x1, Pallas kernels, local(): pl.pallas_call(body, out_shape=jax.ShapeDtypeStruct((n_head, blk, cols),...  122 us

profile of v4, /device:TPU:1, one launch (start us, length us, event | category | flops | bytes accessed | tf_op | source)
XLA Modules:
  0.0 123.5 jit_solution(17457461677808357856)
XLA Ops:
  0.0 121.8 %two_layers.1 = bf16[8,32,512]{2,1,0:T(8,128)(2,1)} custom-call(s32[1,2]{1,0:T(1,128)} %bitcast.17, bf16[8,32,512]{2,1,0:T(8,128)(2,1)} %bitcast.16, bf16[1,512]{1,0:T(2,128)(2,1)} %refs_2_.1, bf16[512,1280]{1,0:T(8,128)(2,1)} %bitcast.12, bf16[1024,512]{1,0:T(8,128)(2,1)} %bitcast.14, bf16[1,512]{1,0:T(2,128)(2,1)} %refs_5_.1, ...), custom_call_target="tpu_custom_call" | custom-call | tf_op jit(solution)/shard_map/two_layers/pallas_call | solution.py:601
  121.8 1.7 %copy.14 = bf16[1,256,512]{2,1,0:T(8,128)(2,1)} copy(bf16[1,256,512]{2,1,0:T(8,128)(2,1)} %bitcast.13) | data formatting | bytes 524288

commit v5 on v4

--- a/solution.py
+++ b/solution.py
@@ -26,7 +26,7 @@
 
 PIECES = 2
 PARTS = (1, 1, 2, 2, 2, 2, 2, 2)
-SETS = ((0, 1, 2, 3), (4, 5), (6, 7))
+SETS = ((0, 1), (2, 3), (4, 5), (6, 7))
 
 
 def split_two(value, lanes):
@@ -600,7 +600,7 @@
 
     out = pl.pallas_call(
         body,
-        out_shape=jax.ShapeDtypeStruct((n_head, blk, cols), BF16),
+        out_shape=pltpu.VMEM((n_head, blk, cols), BF16),
         in_specs=[smem, hbm, vmem, hbm, hbm, vmem, hbm, hbm, hbm, hbm, vmem, vmem],
         out_specs=vmem,
         scratch_shapes=[scratch[name] for name in names],

time: 124 us -> 121 us (0.976)
  no operation moved by 1% of the time
where the time goes in v5:
time: 121 us
  Pallas kernels  121 us (100%)
    pallas_call x1, Pallas kernels, local(): pl.pallas_call(body, out_shape=pltpu.VMEM((n_head, blk, cols), BF16), in_...  121 us

profile of v5, /device:TPU:1, one launch (start us, length us, event | category | flops | bytes accessed | tf_op | source)
XLA Modules:
  0.0 121.3 jit_solution(10085475883428226544)
XLA Ops:
  0.0 120.6 %two_layers.1 = bf16[8,32,512]{2,1,0:T(8,128)(2,1)S(1)} custom-call(s32[1,2]{1,0:T(1,128)} %bitcast.17, bf16[8,32,512]{2,1,0:T(8,128)(2,1)} %bitcast.16, bf16[1,512]{1,0:T(2,128)(2,1)} %refs_2_.1, bf16[512,1280]{1,0:T(8,128)(2,1)} %bitcast.13, bf16[1024,512]{1,0:T(8,128)(2,1)} %bitcast.14, bf16[1,512]{1,0:T(2,128)(2,1)} %refs_5_.1, ...), custom_call_target="tpu_custom_call" | custom-call | tf_op jit(solution)/shard_map/two_layers/pallas_call | solution.py:601
  120.6 0.7 copy.14

commit v6 on v5

--- a/solution.py
+++ b/solution.py
@@ -339,20 +339,18 @@
         den = den + w
         num = num + w * mixed[p, :, qw : qw + HEAD].astype(F32)
     long_out = num / den
-    lhs = s["lhs"]
-    lhs[...] = mixed[:, :, 0:qw]
+    sent("p2", mixed, n_req - 1)
     first = lax.broadcasted_iota(jnp.int32, (16, qw), 0) == 0
     for j in range(2):
         flat = jnp.concatenate([long_out[j * 8 + h : j * 8 + h + 1] for h in range(HEADS)], axis=1)
         block = mixed[j * mid, :, 0:qw].astype(F32)
-        lhs[j * mid] = jnp.where(first, jnp.broadcast_to(flat, (16, qw)), block).astype(BF16)
+        mixed[j * mid, :, 0:qw] = jnp.where(first, jnp.broadcast_to(flat, (16, qw)), block).astype(BF16)
 
     send3, recv3, res = s["send3"], s["recv3"], s["res"]
     for h in range(n_half):
-        part = jnp.dot(lhs[...].reshape(rows, qw), s["wo"][:, pl.ds(h * hcols, hcols)], preferred_element_type=F32)
+        part = jnp.dot(mixed[:, :, 0:qw].reshape(rows, qw), s["wo"][:, pl.ds(h * hcols, hcols)], preferred_element_type=F32)
         send3[h] = part.astype(BF16).reshape(n_head, blk, hcols)
         spread_head("p3", lambda p, h=h: send3.at[h, p], recv3.at[h], h)
-    sent("p2", mixed, n_req - 1)
 
     def block_total(buffer, mine, h):
         value = mine[h, mz].astype(F32)
@@ -504,9 +502,12 @@
     def _():
         for h in range(n_half):
             arrived("p8", out.at[h], n_head - 1, h)
-
-    for h in range(n_half):
-        out_ref[:, :, pl.ds(h * hcols, hcols)] = out[h]
+            out_ref[:, :, pl.ds(h * hcols, hcols)] = out[h]
+
+    @pl.when(sec == 0)
+    def _():
+        for h in range(n_half):
+            out_ref[:, :, pl.ds(h * hcols, hcols)] = out[h]
 
     @pl.when(sec == 1)
     def _():
@@ -567,7 +568,6 @@
         att=pltpu.VMEM((HEADS * 16, HEAD), F32),
         lse=pltpu.VMEM((HEADS * 16, HEAD), F32),
         mixed=pltpu.VMEM((n_req, 16, qw + 2 * HEAD), BF16),
-        lhs=pltpu.VMEM((n_req, 16, qw), BF16),
         send3=pltpu.VMEM(half, BF16),
         recv3=pltpu.VMEM(half, BF16),
         res=pltpu.VMEM(half, BF16),

time: 121 us -> 122 us (level)
  no operation moved by 1% of the time
where the time goes in v6:
time: 122 us
  Pallas kernels  121 us (99%)
    pallas_call x1, Pallas kernels, local(): pl.pallas_call(body, out_shape=pltpu.VMEM((n_head, blk, cols), BF16), in_...  121 us

profile of v6, /device:TPU:1, one launch (start us, length us, event | category | flops | bytes accessed | tf_op | source)
XLA Modules:
  0.0 121.6 jit_solution(12343889160329835572)
XLA Ops:
  0.0 120.9 %two_layers.1 = bf16[8,32,512]{2,1,0:T(8,128)(2,1)S(1)} custom-call(s32[1,2]{1,0:T(1,128)} %bitcast.17, bf16[8,32,512]{2,1,0:T(8,128)(2,1)} %bitcast.16, bf16[1,512]{1,0:T(2,128)(2,1)} %refs_2_.1, bf16[512,1280]{1,0:T(8,128)(2,1)} %bitcast.13, bf16[1024,512]{1,0:T(8,128)(2,1)} %bitcast.14, bf16[1,512]{1,0:T(2,128)(2,1)} %refs_5_.1, ...), custom_call_target="tpu_custom_call" | custom-call | tf_op jit(solution)/shard_map/two_layers/pallas_call | solution.py:601
  120.9 0.7 copy.14
